TPU v7x, 32 devices: a whole 2x2x4 slice. The times are simulated.
32 devices in a mesh: dp: 8 (over y, x, core), ctx: 4 (over z).
Axes of the slice: x: 2, y: 2, z: 4, core: 2. Of those that a mesh axis runs over, the one named last changes fastest.
Arguments:
- tokens: bfloat16 [16, 2048, 1088], P('dp', 'ctx'), may hold values from -6 to 6
- segments: int32 [16, 2048], P('dp'), may hold values from 0 to 31, never falling along the last dimension, each value on 1 to 1024 neighbouring positions
- adapter_index: int32 [16], P('dp'), may hold values from 0 to 7
- w_qkv: bfloat16 [1088, 3264], P('ctx', 'dp'), may hold values from -0.1875 to 0.1875
- w_out: bfloat16 [1088, 1088], P('ctx', 'dp'), may hold values from -0.75 to 0.75
- w_fc1: bfloat16 [1088, 4352], P('ctx', 'dp'), may hold values from -0.1875 to 0.1875
- w_fc2: bfloat16 [4352, 1088], P('ctx', 'dp'), may hold values from -0.09375 to 0.09375
- gain_one: float32 [1088], replicated, may hold values from 0.1 to 1.9
- gain_two: float32 [1088], replicated, may hold values from 0.1 to 1.9
- qkv_down: bfloat16 [128, 1088], replicated, may hold values from -0.1875 to 0.1875
- qkv_up: bfloat16 [128, 3264], replicated, may hold values from -0.75 to 0.75
- out_down: bfloat16 [128, 1088], replicated, may hold values from -0.1875 to 0.1875
- out_up: bfloat16 [128, 1088], replicated, may hold values from -0.75 to 0.75
- fc1_down: bfloat16 [128, 1088], replicated, may hold values from -0.1875 to 0.1875
- fc1_up: bfloat16 [128, 4352], replicated, may hold values from -0.75 to 0.75
- fc2_down: bfloat16 [128, 4352], replicated, may hold values from -0.09375 to 0.09375
- fc2_up: bfloat16 [128, 1088], replicated, may hold values from -0.75 to 0.75
- cotangent: bfloat16 [16, 2048, 1088], P('dp', 'ctx'), may hold values from -6 to 6
Outputs:
- output: bfloat16 [16, 2048, 1088], P('dp', 'ctx')
- input_grad: bfloat16 [16, 2048, 1088], P('dp', 'ctx')
- qkv_down_grad: float32 [128, 1088], P('dp', 'ctx')
- qkv_up_grad: float32 [128, 3264], P('dp', 'ctx')
- out_down_grad: float32 [128, 1088], P('dp', 'ctx')
- out_up_grad: float32 [128, 1088], P('dp', 'ctx')
- fc1_down_grad: float32 [128, 1088], P('dp', 'ctx')
- fc1_up_grad: float32 [128, 4352], P('dp', 'ctx')
- fc2_down_grad: float32 [128, 4352], P('dp', 'ctx')
- fc2_up_grad: float32 [128, 1088], P('dp', 'ctx')
Inputs may be any that keep to these rules, and one draw needn't show every extreme that they name: `segments`: document numbers never fall along a sequence; a document holds at most 1024 tokens.
All inputs are finite; a program needn't handle non-finite values.
Results may differ from a plain program's by a relative error of at most 0.023.
Values may be sent and summed in bfloat16 or wider, within the bound.
No kernel may reach another device: no remote copies, remote signals or barrier semaphores. Data moves between devices by JAX's collectives and lax.ppermute only.
A program may use at most 320 MiB of HBM per device.

v0:
```python
import jax
import jax.numpy as jnp
from jax import lax
from jax.sharding import PartitionSpec as P

HEADS = 17
ADAPTERS = 8


eps = 1e-05
neg_big = -1e30


def norm_rows(vector, gain):
    center = vector - jnp.mean(vector, -1, keepdims=True)
    inv_std = lax.rsqrt(jnp.mean(center * center, -1, keepdims=True) + eps)
    scaled = center * inv_std
    return (scaled * gain, scaled, inv_std)


def norm_back(grad, scaled, inv_std, gain):
    inner = grad * gain
    return inv_std * (
        inner
        - jnp.mean(inner, -1, keepdims=True)
        - scaled * jnp.mean(inner * scaled, -1, keepdims=True)
    )


def select_adapter(picker, stack):
    shaped = stack.reshape(picker.shape[1], stack.shape[0] // picker.shape[1], stack.shape[1])
    return jnp.einsum("sa,arw->srw", picker, shaped, preferred_element_type=jnp.float32).astype(
        jnp.bfloat16
    )


def project(inputs, weight, down_rows, up_rows):
    main_part = jnp.einsum("slw,wv->slv", inputs, weight, preferred_element_type=jnp.float32)
    lowered = jnp.einsum(
        "slw,srw->slr", inputs, down_rows, preferred_element_type=jnp.float32
    ).astype(jnp.bfloat16)
    return (
        main_part
        + jnp.einsum("slr,srv->slv", lowered, up_rows, preferred_element_type=jnp.float32),
        lowered,
    )


def project_back(grad_low, inputs, lowered, weight, down_rows, up_rows):
    grad_in = jnp.einsum("slv,wv->slw", grad_low, weight, preferred_element_type=jnp.float32)
    grad_mid = jnp.einsum(
        "slv,srv->slr", grad_low, up_rows, preferred_element_type=jnp.float32
    ).astype(jnp.bfloat16)
    grad_in = grad_in + jnp.einsum(
        "slr,srw->slw", grad_mid, down_rows, preferred_element_type=jnp.float32
    )
    grad_up = jnp.einsum("slr,slv->srv", lowered, grad_low, preferred_element_type=jnp.float32)
    grad_down = jnp.einsum("slr,slw->srw", grad_mid, inputs, preferred_element_type=jnp.float32)
    return (grad_in, grad_down, grad_up)


def gather_weights(part_qkv, part_out, part_fc1, part_fc2):
    wide_qkv, wide_out, wide_fc1, wide_fc2 = (
        lax.all_gather(part_qkv, "dp", axis=1, tiled=True),
        lax.all_gather(part_out, "dp", axis=1, tiled=True),
        lax.all_gather(part_fc1, "dp", axis=1, tiled=True),
        lax.all_gather(part_fc2, "dp", axis=1, tiled=True),
    )
    return (
        lax.all_gather(wide_qkv, "ctx", axis=0, tiled=True),
        lax.all_gather(wide_out, "ctx", axis=0, tiled=True),
        lax.all_gather(wide_fc1, "ctx", axis=0, tiled=True),
        lax.all_gather(wide_fc2, "ctx", axis=0, tiled=True),
    )


def block_mask(query_pos, query_seg, key_pos, key_seg):
    causal = key_pos[None, None, :] <= query_pos[None, :, None]
    same_doc = key_seg[:, None, :] == query_seg[:, :, None]
    return (causal & same_doc)[:, None]


def per_device(
    tokens,
    segments,
    adapter_index,
    w_qkv,
    w_out,
    w_fc1,
    w_fc2,
    gain_one,
    gain_two,
    qkv_down,
    qkv_up,
    out_down,
    out_up,
    fc1_down,
    fc1_up,
    fc2_down,
    fc2_up,
    cotangent,
):
    seq_count, row_count, width = tokens.shape
    head_dim = width // HEADS
    scale = head_dim ** (-0.5)
    full_qkv, full_out, full_fc1, full_fc2 = gather_weights(w_qkv, w_out, w_fc1, w_fc2)
    picker = (adapter_index[:, None] == jnp.arange(ADAPTERS, dtype=jnp.int32)[None, :]).astype(
        jnp.bfloat16
    )
    stacks = (qkv_down, qkv_up, out_down, out_up, fc1_down, fc1_up, fc2_down, fc2_up)
    chosen = [select_adapter(picker, stack) for stack in stacks]
    first_query = lax.axis_index("ctx") * row_count
    query_pos = first_query + jnp.arange(row_count, dtype=jnp.int32)
    query_seg = lax.dynamic_slice_in_dim(segments, first_query, row_count, 1)
    stream = tokens.astype(jnp.float32)
    normed_one, scaled_one, inv_one = norm_rows(stream, gain_one)
    normed_one = normed_one.astype(jnp.bfloat16)
    merged, lowered_qkv = project(normed_one, full_qkv, chosen[0], chosen[1])
    merged = merged.astype(jnp.bfloat16)
    queries = merged[..., :width].reshape(seq_count, row_count, HEADS, head_dim)
    key_vals = merged[..., width:]

    def attend(state, keys, values, mask):
        peak_old, total, accum = state
        scores = (
            jnp.einsum("sqhd,skhd->shqk", queries, keys, preferred_element_type=jnp.float32) * scale
        )
        scores = jnp.where(mask, scores, neg_big)
        peak_new = jnp.maximum(peak_old, jnp.max(scores, -1))
        expo_term = jnp.where(mask, jnp.exp(scores - peak_new[..., None]), 0.0)
        fade = jnp.exp(peak_old - peak_new)
        total = total * fade + jnp.sum(expo_term, -1)
        accum = accum * jnp.swapaxes(fade, 1, 2)[..., None] + jnp.einsum(
            "shqk,skhd->sqhd",
            expo_term.astype(jnp.bfloat16),
            values,
            preferred_element_type=jnp.float32,
        )
        return (peak_new, total, accum)

    start_state = (
        jnp.full((seq_count, HEADS, row_count), neg_big, jnp.float32),
        jnp.zeros((seq_count, HEADS, row_count), jnp.float32),
        jnp.zeros((seq_count, row_count, HEADS, head_dim), jnp.float32),
    )
    piece = lax.all_gather(key_vals, "ctx", axis=1, tiled=True)
    key_count = piece.shape[1]
    block = 512

    def key_step(turn, inner):
        offset = turn * block
        part = lax.dynamic_slice_in_dim(piece, turn * block, block, 1)
        key_pos = offset + jnp.arange(block, dtype=jnp.int32)
        key_seg = lax.dynamic_slice_in_dim(segments, offset, block, 1)
        mask = block_mask(query_pos, query_seg, key_pos, key_seg)
        keys = part[..., :width].reshape(seq_count, block, HEADS, head_dim)
        values = part[..., width:].reshape(seq_count, block, HEADS, head_dim)
        return attend(inner, keys, values, mask)

    peak_end, total_end, accum_end = lax.fori_loop(0, key_count // block, key_step, start_state)
    attended = (accum_end / jnp.swapaxes(total_end, 1, 2)[..., None]).reshape(
        seq_count, row_count, width
    )
    log_total = peak_end + jnp.log(total_end)
    attended_low = attended.astype(jnp.bfloat16)
    branch, lowered_out = project(attended_low, full_out, chosen[2], chosen[3])
    middle = stream + branch
    normed_two, scaled_two, inv_two = norm_rows(middle, gain_two)
    normed_two = normed_two.astype(jnp.bfloat16)
    hidden, lowered_fc1 = project(normed_two, full_fc1, chosen[4], chosen[5])
    active = jax.nn.gelu(hidden, approximate=True).astype(jnp.bfloat16)
    mlp_out, lowered_fc2 = project(active, full_fc2, chosen[6], chosen[7])
    output = (middle + mlp_out).astype(jnp.bfloat16)
    full_qkv, full_out, full_fc1, full_fc2 = gather_weights(w_qkv, w_out, w_fc1, w_fc2)
    grad_active, grad_fc2_down, grad_fc2_up = project_back(
        cotangent, active, lowered_fc2, full_fc2, chosen[6], chosen[7]
    )
    gelu_value, gelu_pull = jax.vjp(
        lambda inner_in: jax.nn.gelu(inner_in, approximate=True), hidden
    )
    grad_hidden = gelu_pull(grad_active)[0].astype(jnp.bfloat16)
    grad_two, grad_fc1_down, grad_fc1_up = project_back(
        grad_hidden, normed_two, lowered_fc1, full_fc1, chosen[4], chosen[5]
    )
    grad_middle = cotangent.astype(jnp.float32) + norm_back(grad_two, scaled_two, inv_two, gain_two)
    grad_branch = grad_middle.astype(jnp.bfloat16)
    grad_att, grad_out_down, grad_out_up = project_back(
        grad_branch, attended_low, lowered_out, full_out, chosen[2], chosen[3]
    )
    grad_att = grad_att.astype(jnp.bfloat16)
    grad_att_heads = grad_att.reshape(seq_count, row_count, HEADS, head_dim)
    delta = jnp.swapaxes(
        jnp.sum(
            (grad_att.astype(jnp.float32) * attended).reshape(
                seq_count, row_count, HEADS, head_dim
            ),
            -1,
        ),
        1,
        2,
    )
    all_keys = lax.all_gather(key_vals, "ctx", axis=1, tiled=True)
    key_total = all_keys.shape[1]
    back_block = 512

    def back_step(turn, state):
        offset = turn * back_block
        part = lax.dynamic_slice_in_dim(all_keys, offset, back_block, 1)
        key_pos = offset + jnp.arange(back_block, dtype=jnp.int32)
        key_seg = lax.dynamic_slice_in_dim(segments, offset, back_block, 1)
        mask = block_mask(query_pos, query_seg, key_pos, key_seg)
        keys = part[..., :width].reshape(seq_count, back_block, HEADS, head_dim)
        values = part[..., width:].reshape(seq_count, back_block, HEADS, head_dim)
        grad_query, grad_keys = state
        scores = (
            jnp.einsum("sqhd,skhd->shqk", queries, keys, preferred_element_type=jnp.float32) * scale
        )
        probs = jnp.where(mask, jnp.exp(scores - log_total[..., None]), 0.0)
        grad_probs = jnp.einsum(
            "sqhd,skhd->shqk", grad_att_heads, values, preferred_element_type=jnp.float32
        )
        grad_scores = (probs * (grad_probs - delta[..., None])).astype(jnp.bfloat16)
        grad_query = grad_query + jnp.einsum(
            "shqk,skhd->sqhd", grad_scores, keys, preferred_element_type=jnp.float32
        )
        grad_k = (
            jnp.einsum("shqk,sqhd->skhd", grad_scores, queries, preferred_element_type=jnp.float32)
            * scale
        )
        grad_v = jnp.einsum(
            "shqk,sqhd->skhd",
            probs.astype(jnp.bfloat16),
            grad_att_heads,
            preferred_element_type=jnp.float32,
        )
        joined = jnp.concatenate(
            [
                grad_k.reshape(seq_count, back_block, width),
                grad_v.reshape(seq_count, back_block, width),
            ],
            -1,
        )
        return (grad_query, lax.dynamic_update_slice_in_dim(grad_keys, joined, offset, 1))

    back_start = (
        jnp.zeros((seq_count, row_count, HEADS, head_dim), jnp.float32),
        jnp.zeros((seq_count, key_total, 2 * width), jnp.float32),
    )
    grad_query, grad_keys = lax.fori_loop(0, key_total // back_block, back_step, back_start)
    own_key_grads = lax.psum_scatter(
        grad_keys.astype(jnp.bfloat16), "ctx", scatter_dimension=1, tiled=True
    ).astype(jnp.float32)
    grad_merged = jnp.concatenate(
        [(grad_query * scale).reshape(seq_count, row_count, width), own_key_grads], -1
    ).astype(jnp.bfloat16)
    grad_one, grad_qkv_down, grad_qkv_up = project_back(
        grad_merged, normed_one, lowered_qkv, full_qkv, chosen[0], chosen[1]
    )
    input_grad = (grad_middle + norm_back(grad_one, scaled_one, inv_one, gain_one)).astype(
        jnp.bfloat16
    )
    picker_wide = picker.astype(jnp.float32)

    def spread(grad):
        return jnp.einsum("sa,srw->arw", picker_wide, grad).reshape(
            ADAPTERS * grad.shape[1], grad.shape[2]
        )

    term_a, term_b, term_c, term_d, term_e, term_f, term_g, term_h = [
        spread(grad)
        for grad in (
            grad_qkv_down,
            grad_qkv_up,
            grad_out_down,
            grad_out_up,
            grad_fc1_down,
            grad_fc1_up,
            grad_fc2_down,
            grad_fc2_up,
        )
    ]
    part_a, part_b, part_c, part_d, part_e, part_f, part_g, part_h = (
        lax.psum_scatter(
            term_a.astype(jnp.bfloat16), "ctx", scatter_dimension=1, tiled=True
        ).astype(jnp.float32),
        lax.psum_scatter(
            term_b.astype(jnp.bfloat16), "ctx", scatter_dimension=1, tiled=True
        ).astype(jnp.float32),
        lax.psum_scatter(
            term_c.astype(jnp.bfloat16), "ctx", scatter_dimension=1, tiled=True
        ).astype(jnp.float32),
        lax.psum_scatter(
            term_d.astype(jnp.bfloat16), "ctx", scatter_dimension=1, tiled=True
        ).astype(jnp.float32),
        lax.psum_scatter(
            term_e.astype(jnp.bfloat16), "ctx", scatter_dimension=1, tiled=True
        ).astype(jnp.float32),
        lax.psum_scatter(
            term_f.astype(jnp.bfloat16), "ctx", scatter_dimension=1, tiled=True
        ).astype(jnp.float32),
        lax.psum_scatter(
            term_g.astype(jnp.bfloat16), "ctx", scatter_dimension=1, tiled=True
        ).astype(jnp.float32),
        lax.psum_scatter(
            term_h.astype(jnp.bfloat16), "ctx", scatter_dimension=1, tiled=True
        ).astype(jnp.float32),
    )
    final_a, final_b, final_c, final_d, final_e, final_f, final_g, final_h = (
        lax.psum_scatter(part_a.astype(jnp.bfloat16), "dp", scatter_dimension=0, tiled=True).astype(
            jnp.float32
        ),
        lax.psum_scatter(part_b.astype(jnp.bfloat16), "dp", scatter_dimension=0, tiled=True).astype(
            jnp.float32
        ),
        lax.psum_scatter(part_c.astype(jnp.bfloat16), "dp", scatter_dimension=0, tiled=True).astype(
            jnp.float32
        ),
        lax.psum_scatter(part_d.astype(jnp.bfloat16), "dp", scatter_dimension=0, tiled=True).astype(
            jnp.float32
        ),
        lax.psum_scatter(part_e.astype(jnp.bfloat16), "dp", scatter_dimension=0, tiled=True).astype(
            jnp.float32
        ),
        lax.psum_scatter(part_f.astype(jnp.bfloat16), "dp", scatter_dimension=0, tiled=True).astype(
            jnp.float32
        ),
        lax.psum_scatter(part_g.astype(jnp.bfloat16), "dp", scatter_dimension=0, tiled=True).astype(
            jnp.float32
        ),
        lax.psum_scatter(part_h.astype(jnp.bfloat16), "dp", scatter_dimension=0, tiled=True).astype(
            jnp.float32
        ),
    )
    return (
        output,
        input_grad,
        final_a,
        final_b,
        final_c,
        final_d,
        final_e,
        final_f,
        final_g,
        final_h,
    )


def solution(mesh):
    return jax.shard_map(
        per_device,
        mesh=mesh,
        in_specs=(
            P("dp", "ctx", None),
            P("dp", None),
            P("dp"),
            P("ctx", "dp"),
            P("ctx", "dp"),
            P("ctx", "dp"),
            P("ctx", "dp"),
            P(),
            P(),
            P(),
            P(),
            P(),
            P(),
            P(),
            P(),
            P(),
            P(),
            P("dp", "ctx", None),
        ),
        out_specs=(
            P("dp", "ctx", None),
            P("dp", "ctx", None),
            P("dp", "ctx"),
            P("dp", "ctx"),
            P("dp", "ctx"),
            P("dp", "ctx"),
            P("dp", "ctx"),
            P("dp", "ctx"),
            P("dp", "ctx"),
            P("dp", "ctx"),
        ),
        check_vma=False,
    )
```

profile of v0, /device:TPU:9, one launch (start us, length us, event | category | flops | bytes accessed | tf_op | source)
XLA Modules:
  0.0 1881.6 jit_solution(2579130718959137755)
XLA Ops:
  8.0 32.0 %all-gather.23.cloned.1.call-done = bf16[8,408,272]{1,2,0:T(8,128)(2,1)} async-done(((bf16[1,408,272]{1,2,0:T(8,128)(2,1)}), bf16[8,408,272]{1,2,0:T(8,128)(2,1)}) %all-gather.23.cloned.1.call-update) | async-done | bytes 1775632 | tf_op jit(solution)/shard_map/all_gather | solution.py:64
  64.3 112.9 %all-gather.11.cloned.1.call-done = bf16[1088,3264]{1,0:T(8,128)(2,1)} async-done(((bf16[272,3264]{1,0:T(8,128)(2,1)}), bf16[1088,3264]{1,0:T(8,128)(2,1)}) %all-gather.11.cloned.1.call-update) | async-done | bytes 7102480 | tf_op jit(solution)/shard_map/all_gather | solution.py:70
  177.2 12.5 fusion.39
  197.6 15.2 all_gather.39
  257.2 293.5 %all-gather.13.cloned.1.call-done = bf16[2,2048,2176]{1,2,0:T(8,128)(2,1)} async-done(((bf16[2,512,2176]{1,2,0:T(8,128)(2,1)}), bf16[2,2048,2176]{1,2,0:T(8,128)(2,1)}) %all-gather.13.cloned.1.call-update) | async-done | bytes 17825808 | tf_op jit(solution)/shard_map/all_gather | solution.py:146
  550.7 221.1 %while.34 = (s32[]{:T(128)}, f32[2,17,512]{2,1,0:T(8,128)S(1)}, f32[2,17,512]{2,1,0:T(8,128)S(1)}, f32[2,512,17,64]{1,3,2,0:T(8,128)}, s32[2,2048]{1,0:T(2,128)}...) while((s32[]{:T(128)}, f32[2,17,512]{2,1,0:T(8,128)S(1)}, ...), condition=%wide.region_5.6_spmd.clone, body=%wide.region_2.5_spmd.clone.sunk | while | flops 2402327552 | bytes 135225584 | solution.py:160
  556.0 14.8 fusion.239
  570.9 15.3 fusion.241
  586.2 17.9 bitcast_add_fusion.4
  609.6 16.5 fusion.239
  626.2 15.4 fusion.241
  641.6 19.9 %bitcast_add_fusion.4 = f32[2,512,17,64]{1,3,2,0:T(8,128)} fusion(f32[2,512,17,64]{1,3,2,0:T(8,128)} %get-tuple-element.657, f32[2,512,17]{1,2,0:T(8,128)S(1)} %get-tuple-element.623, pred[]{:T(512)S(6)} %compare.6, bf16[2,512,17,64]{1,3,2,0:T(8,128)(2,1)} %bitcast.272, f32[2,17,512,512]{3,2,1,0:T(8,128)} %get-tuple-element.622, ...), kind=kOutput, calls=%fused_computation.9.clone.1 | convolution fusion | flops 1188757504 | bytes 47456256 | tf_op jit(solution)/shard_map/while/body/eval_jaxpr/shqk,skhd->sqhd/dot_general | solution.py:133
  667.0 14.4 fusion.239
  681.4 15.4 fusion.241
  696.8 20.1 %bitcast_add_fusion.4 = f32[2,512,17,64]{1,3,2,0:T(8,128)} fusion(f32[2,512,17,64]{1,3,2,0:T(8,128)} %get-tuple-element.657, f32[2,512,17]{1,2,0:T(8,128)S(1)} %get-tuple-element.623, pred[]{:T(512)S(6)} %compare.6, bf16[2,512,17,64]{1,3,2,0:T(8,128)(2,1)} %bitcast.272, f32[2,17,512,512]{3,2,1,0:T(8,128)} %get-tuple-element.622, ...), kind=kOutput, calls=%fused_computation.9.clone.1 | convolution fusion | flops 1188757504 | bytes 47456256 | tf_op jit(solution)/shard_map/while/body/eval_jaxpr/shqk,skhd->sqhd/dot_general | solution.py:133
  722.4 14.3 fusion.239
  736.7 15.3 fusion.241
  752.0 19.5 %bitcast_add_fusion.4 = f32[2,512,17,64]{1,3,2,0:T(8,128)} fusion(f32[2,512,17,64]{1,3,2,0:T(8,128)} %get-tuple-element.657, f32[2,512,17]{1,2,0:T(8,128)S(1)} %get-tuple-element.623, pred[]{:T(512)S(6)} %compare.6, bf16[2,512,17,64]{1,3,2,0:T(8,128)(2,1)} %bitcast.272, f32[2,17,512,512]{3,2,1,0:T(8,128)} %get-tuple-element.622, ...), kind=kOutput, calls=%fused_computation.9.clone.1 | convolution fusion | flops 1188757504 | bytes 47456256 | tf_op jit(solution)/shard_map/while/body/eval_jaxpr/shqk,skhd->sqhd/dot_general | solution.py:133
  798.8 28.3 %multiply_convert_fusion = (bf16[2,512,4352]{2,1,0:T(8,128)(2,1)}, f32[2,512,4352]{2,1,0:T(8,128)}) fusion(f32[2,512,4352]{2,1,0:T(8,128)} %fusion.97, bf16[2,512,1088]{1,2,0:T(8,128)(2,1)} %copy-done.17, bf16[1088,4352]{1,0:T(8,128)(2,1)} %all-gather.17.cloned.1.call-done), kind=kOutput, calls=%fused_computation.53 | convolution fusion | flops 9741795328 | bytes 56262656 | tf_op jit(solution)/shard_map/slw,wv->slv/dot_general | solution.py:38
  835.2 111.9 %all-gather.21.cloned.1.call-done = bf16[4352,1088]{1,0:T(8,128)(2,1)} async-done(((bf16[1088,1088]{1,0:T(8,128)(2,1)}), bf16[4352,1088]{1,0:T(8,128)(2,1)}) %all-gather.21.cloned.1.call-update) | async-done | bytes 9469968 | tf_op jit(solution)/shard_map/all_gather | solution.py:73
  947.1 26.7 %fusion.30 = bf16[2,512,4352]{2,1,0:T(8,128)(2,1)} fusion(f32[2,512,4352]{2,1,0:T(8,128)} %get-tuple-element.487, f32[2,512,4352]{2,1,0:T(8,128)} %fusion.93, bf16[2,512,1088]{1,2,0:T(8,128)(2,1)} %param.39, bf16[4352,1088]{1,0:T(8,128)(2,1)} %all-gather.21.cloned.1.call-done), kind=kOutput, calls=%fused_computation.52 | convolution fusion | flops 9790816256 | bytes 56262656 | tf_op jit(solution)/shard_map/slv,wv->slw/dot_general | solution.py:50
  984.8 17.0 fusion.159
  1056.7 21.0 %reduce-scatter.64.cloned.1.call-done = bf16[1088,128]{1,0:T(8,128)(2,1)} async-done(((bf16[4352,128]{1,0:T(8,128)(2,1)}), bf16[1088,128]{1,0:T(8,128)(2,1)}) %reduce-scatter.64.cloned.1.call-update) | async-done | bytes 278544
  1089.9 17.0 reduce-scatter.62.cloned.1.call-done
  1115.1 339.0 %while.35 = (s32[]{:T(128)}, f32[2,512,17,64]{1,3,2,0:T(8,128)}, bf16[2,2048,2176]{1,2,0:T(8,128)(2,1)}, bf16[2,2048,2176]{1,2,0:T(8,128)(2,1)}, s32[2,2048]{1,0...) while((s32[]{:T(128)}, f32[2,512,17,64]{1,3,2,0:T(8,128)}, ...), condition=%wide.region_12.13_spmd.clone, body=%wide.region_11.12_spmd.clone.sunk | while | flops 5808063488 | bytes 236294480 | solution.py:249
  1121.6 15.6 fusion.253
  1137.1 16.6 fusion.255
  1153.7 22.1 %fusion.254 = bf16[2,17,512,512]{2,3,1,0:T(8,128)(2,1)} fusion(f32[2,17,512,512]{3,2,1,0:T(8,128)} %fusion.253, bf16[2,512,17,64]{1,3,2,0:T(8,128)(2,1)} %bitcast.274, bf16[2,512,17,64]{1,3,2,0:T(8,128)(2,1)} %get-tuple-element.722, f32[2,17,512]{2,1,0:T(8,128)S(1)} %get-tuple-element.723, f32[2,17,512]{2,1,0:T(8,128)S(1)} %get-tuple-element.721, ...), kind=kOutput, calls=%fused_computation.27.clone.1 | convolution fusion | flops 1194328064 | bytes 58597376 | tf_op jit(solution)/shard_map/while/body/eval_jaxpr/sqhd,skhd->shqk/dot_general | solution.py:219
  1175.8 11.0 bitcast_add_fusion.5
  1186.8 10.0 broadcast_multiply_fusion.8
  1205.3 15.5 fusion.253
  1220.8 16.7 fusion.255
  1237.5 22.0 %fusion.254 = bf16[2,17,512,512]{2,3,1,0:T(8,128)(2,1)} fusion(f32[2,17,512,512]{3,2,1,0:T(8,128)} %fusion.253, bf16[2,512,17,64]{1,3,2,0:T(8,128)(2,1)} %bitcast.274, bf16[2,512,17,64]{1,3,2,0:T(8,128)(2,1)} %get-tuple-element.722, f32[2,17,512]{2,1,0:T(8,128)S(1)} %get-tuple-element.723, f32[2,17,512]{2,1,0:T(8,128)S(1)} %get-tuple-element.721, ...), kind=kOutput, calls=%fused_computation.27.clone.1 | convolution fusion | flops 1194328064 | bytes 58597376 | tf_op jit(solution)/shard_map/while/body/eval_jaxpr/sqhd,skhd->shqk/dot_general | solution.py:219
  1259.5 12.4 bitcast_add_fusion.5
  1290.4 15.6 fusion.253
  1306.0 16.7 fusion.255
  1322.6 22.0 %fusion.254 = bf16[2,17,512,512]{2,3,1,0:T(8,128)(2,1)} fusion(f32[2,17,512,512]{3,2,1,0:T(8,128)} %fusion.253, bf16[2,512,17,64]{1,3,2,0:T(8,128)(2,1)} %bitcast.274, bf16[2,512,17,64]{1,3,2,0:T(8,128)(2,1)} %get-tuple-element.722, f32[2,17,512]{2,1,0:T(8,128)S(1)} %get-tuple-element.723, f32[2,17,512]{2,1,0:T(8,128)S(1)} %get-tuple-element.721, ...), kind=kOutput, calls=%fused_computation.27.clone.1 | convolution fusion | flops 1194328064 | bytes 58597376 | tf_op jit(solution)/shard_map/while/body/eval_jaxpr/sqhd,skhd->shqk/dot_general | solution.py:219
  1344.6 12.2 bitcast_add_fusion.5
  1375.3 15.5 fusion.253
  1390.8 16.5 fusion.255
  1407.4 22.0 %fusion.254 = bf16[2,17,512,512]{2,3,1,0:T(8,128)(2,1)} fusion(f32[2,17,512,512]{3,2,1,0:T(8,128)} %fusion.253, bf16[2,512,17,64]{1,3,2,0:T(8,128)(2,1)} %bitcast.274, bf16[2,512,17,64]{1,3,2,0:T(8,128)(2,1)} %get-tuple-element.722, f32[2,17,512]{2,1,0:T(8,128)S(1)} %get-tuple-element.723, f32[2,17,512]{2,1,0:T(8,128)S(1)} %get-tuple-element.721, ...), kind=kOutput, calls=%fused_computation.27.clone.1 | convolution fusion | flops 1194328064 | bytes 58597376 | tf_op jit(solution)/shard_map/while/body/eval_jaxpr/sqhd,skhd->shqk/dot_general | solution.py:219
  1429.3 12.2 bitcast_add_fusion.5
  1459.3 19.6 %fusion.71 = bf16[2,512,1088]{1,2,0:T(8,128)(2,1)} fusion(f32[2,512,1088]{1,2,0:T(8,128)} %copy-done.7, f32[2,512,1088]{1,2,0:T(8,128)} %fusion.107, bf16[2,512,4352]{2,1,0:T(8,128)(2,1)} %get-tuple-element.486, bf16[4352,1088]{1,0:T(8,128)(2,1)} %all-gather.21.cloned.1.call-done), kind=kOutput, calls=%fused_computation.104 | convolution fusion | flops 9700573184 | bytes 29523968 | tf_op jit(solution)/shard_map/slw,wv->slv/dot_general | solution.py:38
  1487.0 262.0 %reduce-scatter.34.cloned.1.call-done = bf16[2,512,2176]{1,2,0:T(8,128)(2,1)} async-done(((bf16[2,2048,2176]{1,2,0:T(8,128)(2,1)}), bf16[2,512,2176]{1,2,0:T(8,128)(2,1)}) %reduce-scatter.34.cloned.1.call-update) | async-done | bytes 4456464 | tf_op jit(solution)/shard_map/reduce_scatter | solution.py:250
  1763.9 15.1 fusion.158
  1780.7 21.5 %reduce-scatter.54.cloned.1.call-done = bf16[816,128]{1,0:T(8,128)(2,1)} async-done(((bf16[3264,128]{1,0:T(8,128)(2,1)}), bf16[816,128]{1,0:T(8,128)(2,1)}) %reduce-scatter.54.cloned.1.call-update) | async-done | bytes 208912
  1810.4 28.0 %reduce-scatter.36.cloned.1.call-done = bf16[16,272]{1,0:T(8,128)(2,1)} async-done(((bf16[128,272]{1,0:T(8,128)(2,1)}), bf16[16,272]{1,0:T(8,128)(2,1)}) %reduce-scatter.36.cloned.1.call-update) | async-done | bytes 8720 | tf_op jit(solution)/shard_map/reduce_scatter | solution.py:309
  1839.7 33.8 %reduce-scatter.38.cloned.1.call-done = bf16[16,816]{1,0:T(8,128)(2,1)} async-done(((bf16[128,816]{1,0:T(8,128)(2,1)}), bf16[16,816]{1,0:T(8,128)(2,1)}) %reduce-scatter.38.cloned.1.call-update) | async-done | bytes 26128 | tf_op jit(solution)/shard_map/reduce_scatter | solution.py:312
  (370 shorter events, 324.0 us)
Async XLA Ops:
  7.2 232.4 %copy-start = (bf16[128,4352]{1,0:T(8,128)(2,1)S(1)}, bf16[128,4352]{1,0:T(8,128)(2,1)}, u32[]{:S(2)}) copy-start(bf16[128,4352]{1,0:T(8,128)(2,1)} %param.36) | copy-start | bytes 3342340
  7.2 32.8 %all-gather.23.cloned.1.call-start = ((), (), s32[]{:S(2)}) async-start(), calls=%async_computation.32 | async-start | bytes 2506752 | tf_op jit(solution)/shard_map/all_gather | solution.py:64
  7.9 43.2 %copy-start.8 = (bf16[2,512,1088]{1,2,0:T(8,128)(2,1)S(1)}, bf16[2,512,1088]{1,2,0:T(8,128)(2,1)}, u32[]{:S(2)}) copy-start(bf16[2,512,1088]{1,2,0:T(8,128)(2,1)} %param.22) | copy-start | bytes 6684676
  7.9 169.3 %all-gather.11.cloned.1.call-start = ((), (), s32[]{:S(2)}) async-start(), calls=%async_computation.17 | async-start | bytes 9052160 | tf_op jit(solution)/shard_map/all_gather | solution.py:70
  49.4 7.9 copy-start.43
  49.4 165.3 %all-gather.25.cloned.1.call-start = ((), (), s32[]{:S(2)}) async-start(), calls=%async_computation.33 | async-start | bytes 3133440 | tf_op jit(solution)/shard_map/all_gather | solution.py:66
  50.2 201.6 %all-gather.19.cloned.1.call-start = ((), (), s32[]{:S(2)}) async-start(), calls=%async_computation.21 | async-start | bytes 2820096 | tf_op jit(solution)/shard_map/all_gather | solution.py:67
  50.7 499.9 %all-gather.13.cloned.1.call-start = ((), (), s32[]{:S(2)}) async-start(), calls=%async_computation.18 | async-start | bytes 22282240 | tf_op jit(solution)/shard_map/all_gather | solution.py:146
  60.4 129.3 %copy-start.26 = (bf16[2,16,3264]{2,0,1:T(2,128)(2,1)}, bf16[2,16,3264]{2,0,1:T(2,128)(2,1)S(1)}, u32[]{:S(2)}) copy-start(bf16[2,16,3264]{2,0,1:T(2,128)(2,1)S(1)} %convolution_convert_fusion.5) | copy-start | bytes 626692
  64.3 125.4 %copy-start.47 = (bf16[2,512,16]{1,2,0:T(8,128)(2,1)}, bf16[2,512,16]{1,2,0:T(8,128)(2,1)S(1)}, u32[]{:S(2)}) copy-start(bf16[2,512,16]{1,2,0:T(8,128)(2,1)S(1)} %convolution_convert_fusion.21) | copy-start | bytes 98308
  196.7 582.3 %all-gather.15.cloned.1.call-start = ((), (), s32[]{:S(2)}) async-start(), calls=%async_computation.19 | async-start | bytes 3133440 | tf_op jit(solution)/shard_map/all_gather | solution.py:71
  213.9 584.8 %all-gather.17.cloned.1.call-start = ((), (), s32[]{:S(2)}) async-start(), calls=%async_computation.20 | async-start | bytes 11837440 | tf_op jit(solution)/shard_map/all_gather | solution.py:72
  218.6 14.0 copy-start.44
  224.3 18.4 copy-start.19
  224.3 722.8 %all-gather.21.cloned.1.call-start = ((), (), s32[]{:S(2)}) async-start(), calls=%async_computation.22 | async-start | bytes 12533760 | tf_op jit(solution)/shard_map/all_gather | solution.py:73
  242.7 9.0 copy-start.23
  243.1 8.6 copy-start.28
  256.9 293.7 %slice-start = ((bf16[2,512,3264]{1,2,0:T(8,128)(2,1)}), bf16[2,512,1088]{1,2,0:T(8,128)(2,1)S(1)}, s32[]{:S(2)}) async-start(bf16[2,512,3264]{1,2,0:T(8,128)(2,1)} %copy-done.2), calls=%async_computation.42 | async-start | bytes 4456448 | tf_op jit(solution)/shard_map/slice | solution.py:120
  257.0 775.8 %reduce-scatter.66.cloned.1.call-start = ((), (), s32[]{:S(2)}) async-start(), calls=%async_computation.41 | async-start | bytes 348160
  798.8 28.3 %copy-start.24 = (bf16[2,16,4352]{2,0,1:T(2,128)(2,1)S(1)}, bf16[2,16,4352]{2,0,1:T(2,128)(2,1)}, u32[]{:S(2)}) copy-start(bf16[2,16,4352]{2,0,1:T(2,128)(2,1)} %copy-done.23) | copy-start | bytes 835588
  827.0 6.9 copy-start.45
  833.2 140.7 %copy-start.39 = (bf16[2,512,16]{1,2,0:T(8,128)(2,1)}, bf16[2,512,16]{1,2,0:T(8,128)(2,1)S(1)}, u32[]{:S(2)}) copy-start(bf16[2,512,16]{1,2,0:T(8,128)(2,1)S(1)} %convolution_convert_fusion.17) | copy-start | bytes 98308
  835.2 199.3 %reduce-scatter.60.cloned.1.call-start = ((), (), s32[]{:S(2)}) async-start(), calls=%async_computation.38 | async-start | bytes 348160
  984.8 51.5 %reduce-scatter.58.cloned.1.call-start = ((), (), s32[]{:S(2)}) async-start(), calls=%async_computation.37 | async-start | bytes 348160
  984.8 17.1 copy-start.21
  1009.5 37.3 %reduce-scatter.56.cloned.1.call-start = ((), (), s32[]{:S(2)}) async-start(), calls=%async_computation.36 | async-start | bytes 348160
  1014.5 63.2 %reduce-scatter.64.cloned.1.call-start = ((), (), s32[]{:S(2)}) async-start(), calls=%async_computation.40 | async-start | bytes 1392640
  1023.6 83.2 %reduce-scatter.62.cloned.1.call-start = ((), (), s32[]{:S(2)}) async-start(), calls=%async_computation.39 | async-start | bytes 1392640
  1032.7 446.2 %reduce-scatter.50.cloned.1.call-start = ((), (), s32[]{:S(2)}) async-start(), calls=%async_computation.31 | async-start | bytes 110592 | tf_op jit(solution)/shard_map/reduce_scatter | solution.py:330
  1034.4 445.8 %reduce-scatter.44.cloned.1.call-start = ((), (), s32[]{:S(2)}) async-start(), calls=%async_computation.28 | async-start | bytes 110592 | tf_op jit(solution)/shard_map/reduce_scatter | solution.py:321
  1036.2 445.4 %reduce-scatter.42.cloned.1.call-start = ((), (), s32[]{:S(2)}) async-start(), calls=%async_computation.27 | async-start | bytes 110592 | tf_op jit(solution)/shard_map/reduce_scatter | solution.py:318
  1037.9 445.0 %reduce-scatter.40.cloned.1.call-start = ((), (), s32[]{:S(2)}) async-start(), calls=%async_computation.26 | async-start | bytes 110592 | tf_op jit(solution)/shard_map/reduce_scatter | solution.py:315
  1048.5 31.1 %copy-start.32 = (bf16[2,16,1088]{2,0,1:T(2,128)(2,1)S(1)}, bf16[2,16,1088]{2,0,1:T(2,128)(2,1)}, u32[]{:S(2)}) copy-start(bf16[2,16,1088]{2,0,1:T(2,128)(2,1)} %convolution_convert_fusion.14) | copy-start | bytes 208900
  1048.5 31.1 %copy-start.42 = (bf16[2,512,16]{1,2,0:T(8,128)(2,1)S(1)}, bf16[2,512,16]{1,2,0:T(8,128)(2,1)}, u32[]{:S(2)}) copy-start(bf16[2,512,16]{1,2,0:T(8,128)(2,1)} %copy-done.41) | copy-start | bytes 98308
  1048.5 435.7 %reduce-scatter.48.cloned.1.call-start = ((), (), s32[]{:S(2)}) async-start(), calls=%async_computation.30 | async-start | bytes 331776 | tf_op jit(solution)/shard_map/reduce_scatter | solution.py:327
  1079.6 406.0 %reduce-scatter.46.cloned.1.call-start = ((), (), s32[]{:S(2)}) async-start(), calls=%async_computation.29 | async-start | bytes 331776 | tf_op jit(solution)/shard_map/reduce_scatter | solution.py:324
  1108.7 640.3 %reduce-scatter.34.cloned.1.call-start = ((), (), s32[]{:S(2)}) async-start(), calls=%async_computation.23 | async-start | bytes 22282240 | tf_op jit(solution)/shard_map/reduce_scatter | solution.py:250
  1186.8 10.0 copy-start.11
  1271.9 10.0 copy-start.11
  1356.8 9.9 copy-start.11
  1441.6 9.9 copy-start.11
  1454.2 324.8 %reduce-scatter.52.cloned.1.call-start = ((), (), s32[]{:S(2)}) async-start(), calls=%async_computation.34 | async-start | bytes 348160
  1459.3 295.9 %copy-start.25 = (bf16[2,512,17,64]{1,3,2,0:T(8,128)(2,1)}, bf16[2,512,17,64]{1,3,2,0:T(8,128)(2,1)S(1)}, u32[]{:S(2)}) copy-start(bf16[2,512,17,64]{1,3,2,0:T(8,128)(2,1)S(1)} %multiply_convert_fusion.1) | copy-start | bytes 6684676
  1459.3 289.7 %copy-start.27 = (bf16[2,16,3264]{2,0,1:T(2,128)(2,1)S(1)}, bf16[2,16,3264]{2,0,1:T(2,128)(2,1)}, u32[]{:S(2)}) copy-start(bf16[2,16,3264]{2,0,1:T(2,128)(2,1)} %copy-done.26) | copy-start | bytes 626692
  1755.1 47.0 %reduce-scatter.54.cloned.1.call-start = ((), (), s32[]{:S(2)}) async-start(), calls=%async_computation.35 | async-start | bytes 1044480
  1763.8 74.6 %reduce-scatter.36.cloned.1.call-start = ((), (), s32[]{:S(2)}) async-start(), calls=%async_computation.24 | async-start | bytes 110592 | tf_op jit(solution)/shard_map/reduce_scatter | solution.py:309
  1780.6 92.9 %reduce-scatter.38.cloned.1.call-start = ((), (), s32[]{:S(2)}) async-start(), calls=%async_computation.25 | async-start | bytes 258048 | tf_op jit(solution)/shard_map/reduce_scatter | solution.py:312
  1804.0 70.9 %copy-start.1 = (bf16[128,4352]{1,0:T(8,128)(2,1)S(1)}, bf16[128,4352]{1,0:T(8,128)(2,1)}, u32[]{:S(2)}) copy-start(bf16[128,4352]{1,0:T(8,128)(2,1)} %param.36) | copy-start | bytes 3342340
  (44 other events, 125.9 us)
Sparse Core Ops, SparseCore 0:
  9.9 30.0 all-gather.22
  49.5 127.6 all-gather.10
  179.1 35.5 all-gather.24
  216.5 29.6 all-gather.18
  247.6 303.0 all-gather.12
  552.1 51.9 all-gather.14
  605.7 165.2 all-gather.16
  772.5 174.6 all-gather.20
  949.4 16.7 reduce-scatter.65
  984.9 16.7 reduce-scatter.59
  1009.6 16.6 reduce-scatter.57
  1028.4 18.3 reduce-scatter.55
  1049.1 28.5 reduce-scatter.63
  1080.0 26.8 reduce-scatter.61
  1109.7 32.6 reduce-scatter.49
  1145.2 32.4 reduce-scatter.43
  1180.6 32.4 reduce-scatter.41
  1215.9 32.4 reduce-scatter.39
  1251.5 32.8 reduce-scatter.47
  1287.3 32.9 reduce-scatter.45
  1454.3 294.6 reduce-scatter.33
  1755.3 19.6 reduce-scatter.51
  1778.0 24.1 reduce-scatter.53
  1805.0 33.3 reduce-scatter.35
  1841.5 31.9 reduce-scatter.37
where the time goes:
time: 1890 us; the launch traced here: 1880 us
  waiting for transfers between devices  945 us (50%)
  matrix products  665 us (35%)
  local copies, waits for them, and re-layouts  129 us (7%)
  other arithmetic  109 us (6%)
    all_gather x1, waiting for transfers between devices, per_device(): piece = lax.all_gather(key_vals, 'ctx', axis=1, tiled=True)  293 us
    reduce_scatter x1, waiting for transfers between devices, per_device(): lax.psum_scatter(grad_keys.astype(jnp.bfloat16), 'ctx', scatter_dimension...  262 us
    all_gather x1, waiting for transfers between devices, gather_weights(): lax.all_gather(wide_qkv, 'ctx', axis=0, tiled=True)  113 us
    all_gather x1, waiting for transfers between devices, gather_weights(): lax.all_gather(wide_fc2, 'ctx', axis=0, tiled=True)  112 us
    dot_general x4, matrix products, back_step(): jnp.einsum('sqhd,skhd->shqk', grad_att_heads, values, preferred_element_t...  88.1 us
    dot_general x4, matrix products, attend(): jnp.einsum('shqk,skhd->sqhd', expo_term.astype(jnp.bfloat16), values, pre...  77.4 us
    unnamed x33, waiting for transfers between devices  70.7 us
    dot_general x4, matrix products, project_back(): jnp.einsum('slv,wv->slw', grad_low, weight, preferred_element_type=jnp.fl...  67 us
  transfers between devices with their start and end apart: 25, of which 12 were waited for; matrix products, arithmetic and copies ran while one was open for 46% of the time, Pallas kernels for 0%

commit v1 on v0

v1 whole, which is shorter than its diff:
```python
import functools

import jax
import jax.numpy as jnp
from jax import lax
from jax.experimental import pallas as pl
from jax.experimental.pallas import tpu as pltpu
from jax.sharding import PartitionSpec as P

HEADS = 17
ADAPTERS = 8
eps = 1e-05
neg_big = -1e30
BF = jnp.bfloat16
F32 = jnp.float32
BLK = 256
VMEM_LIMIT = 66000000


def nt(a, b):
    return lax.dot_general(a, b, (((1,), (1,)), ((), ())), preferred_element_type=F32)


def nn(a, b):
    return lax.dot_general(a, b, (((1,), (0,)), ((), ())), preferred_element_type=F32)


def tn(a, b):
    return lax.dot_general(a, b, (((0,), (0,)), ((), ())), preferred_element_type=F32)


def norm_rows(vector, gain):
    center = vector - jnp.mean(vector, -1, keepdims=True)
    inv_std = lax.rsqrt(jnp.mean(center * center, -1, keepdims=True) + eps)
    scaled = center * inv_std
    return (scaled * gain, scaled, inv_std)


def norm_back(grad, scaled, inv_std, gain):
    inner = grad * gain
    return inv_std * (
        inner
        - jnp.mean(inner, -1, keepdims=True)
        - scaled * jnp.mean(inner * scaled, -1, keepdims=True)
    )


def mask_bias(start_row, key_base, query_base, size):
    key_pos = lax.broadcasted_iota(jnp.int32, (size, size), 0) + key_base
    query_pos = lax.broadcasted_iota(jnp.int32, (size, size), 1) + query_base
    allowed = (key_pos >= start_row) & (key_pos <= query_pos)
    return jnp.where(allowed, 0.0, neg_big)


def attention_forward_kernel(
    parts, heads, head_dim, blk, first_ref, part_ref, start_ref, *refs
):
    pieces = refs[:parts]
    mixed_ref, flipped_ref, lse_ref = refs[parts : parts + 3]
    turned, keys, peak, total, accum = refs[parts + 3 :]
    wide = heads * head_dim
    local = pieces[0].shape[0]
    scale = head_dim ** (-0.5)
    for i in range(parts):
        base = part_ref[i] * local

        def load(c, _, i=i, base=base):
            rows = pl.ds(pl.multiple_of(c * blk, blk), blk)
            spot = pl.ds(pl.multiple_of(base + c * blk, blk), blk)
            block = pieces[i][rows, :]
            flip = block.T
            turned[:wide, spot] = flip[:wide] * scale
            turned[wide:, spot] = flip[2 * wide :]
            for h in range(heads):
                keys[h, spot, :] = block[:, wide + h * head_dim : wide + (h + 1) * head_dim]
            return 0

        lax.fori_loop(0, local // blk, load, 0)

    def query_block(i, _):
        cols = pl.ds(pl.multiple_of(i * blk, blk), blk)
        start_row = start_ref[:, cols]

        def visit(j, fresh):
            rows = pl.ds(pl.multiple_of(j * blk, blk), blk)
            bias = mask_bias(start_row, j * blk, i * blk, blk)
            for h in range(heads):
                band = slice(h * head_dim, (h + 1) * head_dim)
                below = slice(wide + h * head_dim, wide + (h + 1) * head_dim)
                scores = nn(keys[h, rows, :], turned[band, cols]) + bias
                top = jnp.max(scores, 0, keepdims=True)
                if fresh:
                    expo = jnp.exp(scores - top)
                    peak[h] = top
                    total[h] = jnp.sum(expo, 0, keepdims=True)
                    accum[band, :] = nn(turned[below, rows], expo.astype(BF))
                else:
                    old = peak[h]
                    new = jnp.maximum(old, top)
                    fade = jnp.exp(old - new)
                    expo = jnp.exp(scores - new)
                    peak[h] = new
                    total[h] = total[h] * fade + jnp.sum(expo, 0, keepdims=True)
                    accum[band, :] = accum[band, :] * fade + nn(
                        turned[below, rows], expo.astype(BF)
                    )

        visit(i, True)

        def more(k, _):
            visit(i - 1 - k, False)
            return 0

        lax.fori_loop(0, i - first_ref[i], more, 0)
        for h in range(heads):
            band = slice(h * head_dim, (h + 1) * head_dim)
            sums = total[h]
            lse_ref[h, :, cols] = peak[h] + jnp.log(sums)
            accum[band, :] = accum[band, :] * (1.0 / sums)
        low = accum[...].astype(BF)
        flipped_ref[:, cols] = low
        mixed_ref[cols, :] = low.T
        return 0

    lax.fori_loop(0, mixed_ref.shape[0] // blk, query_block, 0)


def attention_backward_kernel(
    parts, heads, head_dim, blk, first_ref, part_ref, start_ref, lse_ref, flipped_ref, *refs
):
    pieces = refs[:parts]
    grads = refs[parts : 2 * parts]
    out_ref = refs[2 * parts]
    turned, keys, values, grad_turned, delta, dq, dk, dv = refs[2 * parts + 1 :]
    wide = heads * head_dim
    local = pieces[0].shape[0]
    scale = head_dim ** (-0.5)
    for i in range(parts):
        base = part_ref[i] * local

        def load(c, _, i=i, base=base):
            rows = pl.ds(pl.multiple_of(c * blk, blk), blk)
            spot = pl.ds(pl.multiple_of(base + c * blk, blk), blk)
            block = pieces[i][rows, :]
            flip = block[:, : 2 * wide].T
            turned[:wide, spot] = flip[:wide] * scale
            turned[wide:, spot] = flip[wide:]
            gflip = grads[i][rows, :].T
            grad_turned[:, spot] = gflip
            product = gflip.astype(F32) * flipped_ref[:, spot].astype(F32)
            for h in range(heads):
                band = slice(h * head_dim, (h + 1) * head_dim)
                keys[h, spot, :] = block[:, wide + h * head_dim : wide + (h + 1) * head_dim]
                values[h, spot, :] = block[
                    :, 2 * wide + h * head_dim : 2 * wide + (h + 1) * head_dim
                ]
                delta[h, :, spot] = jnp.sum(product[band], 0, keepdims=True)
            return 0

        lax.fori_loop(0, local // blk, load, 0)
    dk[...] = jnp.zeros_like(dk)
    dv[...] = jnp.zeros_like(dv)

    def query_block(i, _):
        cols = pl.ds(pl.multiple_of(i * blk, blk), blk)
        start_row = start_ref[:, cols]
        dq[:, cols] = jnp.zeros((wide, blk), F32)

        def visit(k, _):
            j = i - k
            rows = pl.ds(pl.multiple_of(j * blk, blk), blk)
            bias = mask_bias(start_row, j * blk, i * blk, blk)
            for h in range(heads):
                band = slice(h * head_dim, (h + 1) * head_dim)
                below = slice(wide + h * head_dim, wide + (h + 1) * head_dim)
                queries = turned[band, cols]
                out_grad = grad_turned[band, cols]
                scores = nn(keys[h, rows, :], queries) + bias
                probs = jnp.exp(scores - lse_ref[h, :, cols])
                grad_probs = nn(values[h, rows, :], out_grad)
                grad_scores = (probs * (grad_probs - delta[h, :, cols])).astype(BF)
                dq[band, cols] += nn(turned[below, rows], grad_scores)
                dk[band, rows] += nt(queries, grad_scores)
                dv[band, rows] += nt(out_grad, probs.astype(BF))
            return 0

        lax.fori_loop(0, i - first_ref[i] + 1, visit, 0)
        return 0

    lax.fori_loop(0, start_ref.shape[1] // blk, query_block, 0)

    def finish(c, _):
        spot = pl.ds(pl.multiple_of(c * blk, blk), blk)
        out_ref[spot, :] = jnp.concatenate(
            [
                (dq[:, spot] * scale).astype(BF),
                dk[:, spot].astype(BF),
                dv[:, spot].astype(BF),
            ],
            0,
        ).T
        return 0

    lax.fori_loop(0, start_ref.shape[1] // blk, finish, 0)


def attention_forward(first, part_ids, start_row, pieces, heads, head_dim):
    parts, length = len(pieces), start_row.shape[1]
    wide = heads * head_dim
    blk = min(BLK, pieces[0].shape[0])
    smem, vmem = pl.BlockSpec(memory_space=pltpu.SMEM), pl.BlockSpec(memory_space=pltpu.VMEM)
    area = heads * length * 640
    return pl.pallas_call(
        functools.partial(attention_forward_kernel, parts, heads, head_dim, blk),
        out_shape=(
            jax.ShapeDtypeStruct((length, wide), BF),
            jax.ShapeDtypeStruct((wide, length), BF),
            jax.ShapeDtypeStruct((heads, 1, length), F32),
        ),
        in_specs=[smem, smem] + [vmem] * (1 + parts),
        out_specs=(vmem, vmem, vmem),
        scratch_shapes=[
            pltpu.VMEM((2 * wide, length), BF),
            pltpu.VMEM((heads, length, head_dim), BF),
            pltpu.VMEM((heads, 1, blk), F32),
            pltpu.VMEM((heads, 1, blk), F32),
            pltpu.VMEM((wide, blk), F32),
        ],
        compiler_params=pltpu.CompilerParams(vmem_limit_bytes=VMEM_LIMIT),
        cost_estimate=pl.CostEstimate(
            flops=area * 1024, bytes_accessed=10 * length * wide, transcendentals=area
        ),
        name="attention_forward",
    )(first, part_ids, start_row, *pieces)


def attention_backward(first, part_ids, start_row, lse, flipped, pieces, grads, heads, head_dim):
    parts, length = len(pieces), start_row.shape[1]
    wide = heads * head_dim
    blk = min(BLK, pieces[0].shape[0])
    smem, vmem = pl.BlockSpec(memory_space=pltpu.SMEM), pl.BlockSpec(memory_space=pltpu.VMEM)
    area = heads * length * 640
    return pl.pallas_call(
        functools.partial(attention_backward_kernel, parts, heads, head_dim, blk),
        out_shape=jax.ShapeDtypeStruct((length, 3 * wide), BF),
        in_specs=[smem, smem] + [vmem] * (3 + 2 * parts),
        out_specs=vmem,
        scratch_shapes=[
            pltpu.VMEM((2 * wide, length), BF),
            pltpu.VMEM((heads, length, head_dim), BF),
            pltpu.VMEM((heads, length, head_dim), BF),
            pltpu.VMEM((wide, length), BF),
            pltpu.VMEM((heads, 1, length), F32),
            pltpu.VMEM((wide, length), F32),
            pltpu.VMEM((wide, length), F32),
            pltpu.VMEM((wide, length), F32),
        ],
        compiler_params=pltpu.CompilerParams(vmem_limit_bytes=VMEM_LIMIT),
        cost_estimate=pl.CostEstimate(
            flops=area * 2560, bytes_accessed=16 * length * wide, transcendentals=area
        ),
        name="attention_backward",
    )(first, part_ids, start_row, lse, flipped, *pieces, *grads)


def per_device(
    dp_size,
    ctx_size,
    tokens,
    segments,
    adapter_index,
    w_qkv,
    w_out,
    w_fc1,
    w_fc2,
    gain_one,
    gain_two,
    qkv_down,
    qkv_up,
    out_down,
    out_up,
    fc1_down,
    fc1_up,
    fc2_down,
    fc2_up,
    cotangent,
):
    both = ("dp", "ctx")
    seqs, rows, width = tokens.shape
    length = segments.shape[1]
    head_dim = width // HEADS
    rank = qkv_down.shape[0] // ADAPTERS
    group = ctx_size // seqs
    local = seqs * rows
    heads = -(-HEADS // group)
    wide = heads * head_dim
    ratio = w_fc2.shape[0] // w_fc1.shape[0]
    cut = w_fc1.shape[0]
    hidden_size = fc1_up.shape[1]

    dp_at, ctx_at = lax.axis_index("dp"), lax.axis_index("ctx")
    core_at = dp_at % 2
    place = ctx_at * 2 + core_at
    seq_at, part_at = place // group, place % group

    def send(value, route):
        pairs = []
        for d in range(dp_size):
            for z in range(ctx_size):
                d2, z2 = route(d, z)
                pairs.append((d * ctx_size + z, d2 * ctx_size + z2))
        return lax.ppermute(value, both, pairs)

    def to_sequence(p):
        def route(d, z):
            q = (d % 2) * seqs + (z + p) % seqs
            e = q * group + z // seqs
            return (d // 2) * 2 + e % 2, e // 2

        return route

    def from_sequence(p):
        def route(d, z):
            e = 2 * z + d % 2
            q, r = e // group, e % group
            t = (q - p) % seqs
            return (d // 2) * 2 + q // seqs, r * seqs + t

        return route

    def within_group(m):
        def route(d, z):
            e = 2 * z + d % 2
            e2 = (e // group) * group + (e % group ^ m)
            return (d // 2) * 2 + e2 % 2, e2 // 2

        return route

    def pick(stack, index):
        return lax.dynamic_index_in_dim(stack, index, 0, keepdims=False)

    def spread_tokens(block):
        got = [
            send(pick(block, (ctx_at + p) % seqs), to_sequence(p)) for p in range(seqs)
        ]
        stacked = jnp.stack(got)
        return jnp.concatenate(
            [pick(stacked, (seq_at - t) % seqs) for t in range(seqs)], 0
        )

    def return_tokens(block):
        shaped = block.reshape(seqs, rows, width)
        got = [
            send(pick(shaped, (seq_at - p) % seqs), from_sequence(p)) for p in range(seqs)
        ]
        stacked = jnp.stack(got)
        return jnp.stack([pick(stacked, (j - ctx_at) % seqs) for j in range(seqs)])

    def gather_rows(shard):
        got = [shard] + [
            send(shard, lambda d, z, k=k: (d, (z + k) % ctx_size))
            for k in range(1, ctx_size)
        ]
        cycle = jnp.stack(got[:0:-1] + got[:1] + got[:0:-1])
        ordered = lax.dynamic_slice_in_dim(cycle, ctx_size - 1 - ctx_at, ctx_size, 0)
        return ordered.reshape(ctx_size * shard.shape[0], shard.shape[1]).T

    plane_bits = []
    bit = 2
    while bit < dp_size:
        plane_bits.append(bit)
        bit *= 2
    half_bits = len(plane_bits) // 2

    def join(mine, other, bit):
        low = (dp_at // bit) % 2 == 0
        return jnp.stack([jnp.where(low, mine, other), jnp.where(low, other, mine)])

    def gather_columns(block):
        n = block.shape[0]
        first = -(-n // 16) * 8
        done = []
        for piece, order in (
            (block[:first], plane_bits),
            (block[first:], plane_bits[half_bits:] + plane_bits[:half_bits]),
        ):
            held, axes = piece[None], []
            for b in order:
                other = send(held, lambda d, z, b=b: (d ^ b, z))
                held = join(held, other, b)
                axes = [b] + axes
                held = held.reshape((2,) * len(axes) + piece.shape)
            wanted = sorted(axes, reverse=True)
            held = held.transpose([axes.index(b) for b in wanted] + [len(axes), len(axes) + 1])
            done.append(held.reshape((dp_size // 2,) + piece.shape))
        held = jnp.concatenate(done, 1)
        other = send(held, lambda d, z: (d ^ 1, z))
        low = core_at == 0
        return jnp.stack([jnp.where(low, held, other), jnp.where(low, other, held)], 1).reshape(
            dp_size, n, width
        )

    turned_qkv = gather_columns(gather_rows(w_qkv)).reshape(-1, width)
    sequence_in = spread_tokens(tokens)
    cols_out, cols_fc1, cols_fc2 = w_out.shape[1], w_fc1.shape[1], w_fc2.shape[1]
    rest_shard = jnp.concatenate(
        [w_out, w_fc1]
        + [w_fc2[b * cut : (b + 1) * cut] for b in range(ratio)],
        1,
    )
    rest = gather_columns(gather_rows(rest_shard))
    turned_out = rest[:, :cols_out].reshape(-1, width)
    turned_fc1 = (
        rest[:, cols_out : cols_out + cols_fc1]
        .reshape(ctx_size, ratio, cut, width)
        .transpose(1, 0, 2, 3)
        .reshape(hidden_size, width)
    )
    at = cols_out + cols_fc1
    turned_fc2 = [
        rest[:, at + b * cols_fc2 : at + (b + 1) * cols_fc2].reshape(width, width)
        for b in range(ratio)
    ]

    table = jnp.concatenate([segments, adapter_index[:, None]], 1)
    other_table = send(table, lambda d, z: (d ^ 1, z))
    low = core_at == 0
    tables = jnp.concatenate(
        [jnp.where(low, table, other_table), jnp.where(low, other_table, table)], 0
    )
    own_table = pick(tables, seq_at)
    seg, adapter = own_table[:length], own_table[length]
    column_adapters = tables[:, length]
    start_row = jnp.sum(
        (seg[:, None] < seg[None, :]).astype(jnp.int32), 0, dtype=jnp.int32
    )[None]
    blk = min(BLK, local)
    first = start_row[0, ::blk] // blk
    part_ids = jnp.stack([part_at ^ m for m in range(group)]).astype(jnp.int32)

    def chosen(stack):
        return lax.dynamic_slice_in_dim(stack, adapter * rank, rank, 0)

    d_qkv, u_qkv, d_out, u_out, d_fc1, u_fc1, d_fc2, u_fc2 = [
        chosen(s)
        for s in (qkv_down, qkv_up, out_down, out_up, fc1_down, fc1_up, fc2_down, fc2_up)
    ]

    def by_group(matrix):
        tail = matrix.shape[1]
        shaped = matrix.reshape(3, HEADS, head_dim, tail)
        shaped = jnp.pad(shaped, ((0, 0), (0, group * heads - HEADS), (0, 0), (0, 0)))
        return (
            shaped.reshape(3, group, wide, tail)
            .transpose(1, 0, 2, 3)
            .reshape(group, 3 * wide, tail)
        )

    grouped_qkv = by_group(turned_qkv)
    grouped_up = by_group(u_qkv.T)

    def by_block(matrix):
        return (
            matrix.reshape(rank, ctx_size, ratio, cut)
            .transpose(0, 2, 1, 3)
            .reshape(rank, hidden_size)
        )

    u_fc1, d_fc2 = by_block(u_fc1), by_block(d_fc2)

    stream = sequence_in.astype(F32)
    normed_one, scaled_one, inv_one = norm_rows(stream, gain_one)
    normed_one = normed_one.astype(BF)
    low_qkv = nt(normed_one, d_qkv).astype(BF)
    merged = jnp.stack(
        [
            (nt(normed_one, grouped_qkv[g]) + nt(low_qkv, grouped_up[g])).astype(BF)
            for g in range(group)
        ]
    )
    pieces = [pick(merged, part_at)] + [
        send(pick(merged, part_at ^ m), within_group(m)) for m in range(1, group)
    ]
    mixed, flipped, lse = attention_forward(first, part_ids, start_row, pieces, heads, head_dim)
    mixed = mixed.reshape(group, local, wide)

    def collect(parts_of):
        got = [pick(parts_of, part_at)] + [
            send(pick(parts_of, part_at ^ m), within_group(m)) for m in range(1, group)
        ]
        stacked = jnp.stack(got)
        return [pick(stacked, part_at ^ g) for g in range(group)]

    attended = jnp.concatenate(collect(mixed), 1)[:, :width]
    low_out = nt(attended, d_out).astype(BF)
    middle = stream + nt(attended, turned_out) + nn(low_out, u_out)
    normed_two, scaled_two, inv_two = norm_rows(middle, gain_two)
    normed_two = normed_two.astype(BF)
    low_fc1 = nt(normed_two, d_fc1).astype(BF)
    hidden = nt(normed_two, turned_fc1) + nn(low_fc1, u_fc1)
    active = jax.nn.gelu(hidden, approximate=True).astype(BF)
    low_fc2 = nt(active, d_fc2).astype(BF)
    mlp = nn(low_fc2, u_fc2)
    for b in range(ratio):
        mlp = mlp + nt(active[:, b * width : (b + 1) * width], turned_fc2[b])
    output = return_tokens((middle + mlp).astype(BF))

    grad_out = spread_tokens(cotangent)
    grad_low_fc2 = nt(grad_out, u_fc2).astype(BF)
    grad_active = jnp.concatenate(
        [nn(grad_out, turned_fc2[b]) for b in range(ratio)], 1
    ) + nn(grad_low_fc2, d_fc2)
    grad_fc2_up = tn(low_fc2, grad_out)
    grad_fc2_down = tn(grad_low_fc2, active)
    _, gelu_pull = jax.vjp(lambda v: jax.nn.gelu(v, approximate=True), hidden)
    grad_hidden = gelu_pull(grad_active)[0].astype(BF)
    grad_low_fc1 = nt(grad_hidden, u_fc1).astype(BF)
    grad_two = nn(grad_hidden, turned_fc1) + nn(grad_low_fc1, d_fc1)
    grad_fc1_up = tn(low_fc1, grad_hidden)
    grad_fc1_down = tn(grad_low_fc1, normed_two)
    grad_middle = grad_out.astype(F32) + norm_back(grad_two, scaled_two, inv_two, gain_two)
    grad_branch = grad_middle.astype(BF)
    grad_low_out = nt(grad_branch, u_out).astype(BF)
    grad_att = (nn(grad_branch, turned_out) + nn(grad_low_out, d_out)).astype(BF)
    grad_out_up = tn(low_out, grad_branch)
    grad_out_down = tn(grad_low_out, attended)

    padded = jnp.pad(grad_att, ((0, 0), (0, group * wide - width)))
    by_heads = padded.reshape(local, group, wide).transpose(1, 0, 2)
    grad_pieces = [pick(by_heads, part_at)] + [
        send(pick(by_heads, part_at ^ m), within_group(m)) for m in range(1, group)
    ]
    grad_parts = attention_backward(
        first, part_ids, start_row, lse, flipped, pieces, grad_pieces, heads, head_dim
    ).reshape(group, local, 3 * wide)
    grad_groups = collect(grad_parts)
    grad_low_qkv = sum(nn(grad_groups[g], grouped_up[g]) for g in range(group)).astype(BF)
    grad_one = nn(grad_low_qkv, d_qkv)
    for g in range(group):
        grad_one = grad_one + nn(grad_groups[g], grouped_qkv[g])
    grad_qkv_down = tn(grad_low_qkv, normed_one)
    up_groups = jnp.stack([tn(low_qkv, grad_groups[g]) for g in range(group)], 1)
    grad_qkv_up = (
        up_groups.reshape(rank, group, 3, wide)
        .transpose(0, 2, 1, 3)
        .reshape(rank, 3, group * wide)[:, :, :width]
        .reshape(rank, 3 * width)
    )
    input_grad = return_tokens(
        (grad_middle + norm_back(grad_one, scaled_one, inv_one, gain_one)).astype(BF)
    )

    def plain(grad):
        return grad.reshape(rank, ctx_size, grad.shape[1] // ctx_size).transpose(1, 0, 2)

    def blocked(grad):
        return (
            grad.reshape(rank, ratio, ctx_size, cut)
            .transpose(2, 0, 1, 3)
            .reshape(ctx_size, rank, ratio * cut)
        )

    owners = jnp.stack(
        [
            pick(column_adapters, (((ctx_at - k) % ctx_size) * 2 + core_at) // group)
            for k in range(ctx_size)
        ]
    )
    onehot = (owners[:, None] == jnp.arange(ADAPTERS, dtype=jnp.int32)[None]).astype(F32)

    def reduce_terms(terms):
        packed = jnp.concatenate(terms, 2).astype(BF)
        got = [pick(packed, ctx_at)] + [
            send(
                pick(packed, (ctx_at + k) % ctx_size),
                lambda d, z, k=k: (d, (z + k) % ctx_size),
            )
            for k in range(1, ctx_size)
        ]
        laid = sum(
            onehot[k][:, None, None] * got[k].astype(F32)[None] for k in range(ctx_size)
        ).reshape(dp_size, ADAPTERS * rank // dp_size, packed.shape[2])
        mine = pick(laid, dp_at)
        low_laid = laid.astype(BF)
        for m in range(1, dp_size):
            mine = mine + send(
                pick(low_laid, dp_at ^ m), lambda d, z, m=m: (d ^ m, z)
            ).astype(F32)
        sizes = [t.shape[2] for t in terms]
        ends = [sum(sizes[: i + 1]) for i in range(len(sizes))]
        return [mine[:, e - s : e] for e, s in zip(ends, sizes)]

    od, ou, f1d, f1u, f2d, f2u = reduce_terms(
        [
            plain(grad_out_down),
            plain(grad_out_up),
            plain(grad_fc1_down),
            blocked(grad_fc1_up),
            blocked(grad_fc2_down),
            plain(grad_fc2_up),
        ]
    )
    qd, qu = reduce_terms([plain(grad_qkv_down), plain(grad_qkv_up)])
    return (output, input_grad, qd, qu, od, ou, f1d, f1u, f2d, f2u)


def solution(mesh):
    shape = dict(mesh.shape)
    return jax.shard_map(
        functools.partial(per_device, shape["dp"], shape["ctx"]),
        mesh=mesh,
        in_specs=(
            P("dp", "ctx", None),
            P("dp", None),
            P("dp"),
            P("ctx", "dp"),
            P("ctx", "dp"),
            P("ctx", "dp"),
            P("ctx", "dp"),
        )
        + (P(),) * 10
        + (P("dp", "ctx", None),),
        out_specs=(P("dp", "ctx", None), P("dp", "ctx", None)) + (P("dp", "ctx"),) * 8,
        check_vma=False,
    )
```

time: 1890 us -> 999 us (0.53)
  waiting for transfers between devices: 945 us -> 223 us
  matrix products: 665 us -> 191 us
  Pallas kernels: 0 us -> 134 us
  local copies, waits for them, and re-layouts: 129 us -> 256 us
  starting transfers between devices: 2.12 us -> 73.1 us
    all_gather x8 -> x0, waiting for transfers between devices: 551 us -> none  [the longest x1 293 us: per_device(): piece = lax.all_gather(key_vals, 'ctx', axis=1, tiled=True)]
    dot_general x76 -> x43, matrix products: 665 us -> 191 us  [the longest x17 112 us: nn(): lax.dot_general(a, b, (((1,), (0,)), ((), ())), preferred_element_type=F32)]
    reduce_scatter x9 -> x0, waiting for transfers between devices: 324 us -> none  [the longest x1 262 us: per_device(): lax.psum_scatter(grad_keys.astype(jnp.bfloat16), 'ctx', scatter_dimension...]
    ppermute x0 -> x49, waiting for transfers between devices: none -> 223 us  [send(): return lax.ppermute(value, both, pairs)]
    pallas_call x0 -> x2, Pallas kernels: none -> 134 us  [the longest x1 72.3 us: attention_backward(): pl.pallas_call(functools.partial(attention_backward_kernel, parts, heads,...]
    ppermute x0 -> x49, starting transfers between devices: none -> 73.1 us  [send(): return lax.ppermute(value, both, pairs)]
    unnamed x33 -> x0, waiting for transfers between devices: 70.7 us -> none
    reduce_sum x5 -> x1, other arithmetic: 64.4 us -> 1.7 us  [per_device(): jnp.sum((seg[:, None] < seg[None, :]).astype(jnp.int32), 0, dtype=jnp.int32)]
  transfers between devices with their start and end apart: 25 -> 49, of which waited for: 12 -> 15; matrix products, arithmetic and copies ran while one was open for 46% -> 23% of each run, Pallas kernels for 0% -> 6%
where the time goes in v1:
time: 999 us; the launch traced here: 987 us
  local copies, waits for them, and re-layouts  256 us (26%)
  waiting for transfers between devices  223 us (22%)
  matrix products  191 us (19%)
  Pallas kernels  134 us (13%)
  other arithmetic  106 us (11%)
  starting transfers between devices  73.1 us (7%)
    ppermute x49, waiting for transfers between devices, send(): return lax.ppermute(value, both, pairs)  223 us
    dot_general x17, matrix products, nn(): lax.dot_general(a, b, (((1,), (0,)), ((), ())), preferred_element_type=F32)  112 us
    ppermute x49, starting transfers between devices, send(): return lax.ppermute(value, both, pairs)  73.1 us
    pallas_call x1, Pallas kernels, attention_backward(): pl.pallas_call(functools.partial(attention_backward_kernel, parts, heads,...  72.3 us
    dot_general x17, matrix products, nt(): lax.dot_general(a, b, (((1,), (1,)), ((), ())), preferred_element_type=F32)  63.4 us
    pallas_call x1, Pallas kernels, attention_forward(): pl.pallas_call(functools.partial(attention_forward_kernel, parts, heads,...  61.4 us
    unnamed x256, local copies, waits for them, and re-layouts  49.4 us
    slice x5, local copies, waits for them, and re-layouts, per_device(): rest[:, at + b * cols_fc2:at + (b + 1) * cols_fc2].reshape(width, width)  46.9 us
  transfers between devices with their start and end apart: 49, of which 15 were waited for; matrix products, arithmetic and copies ran while one was open for 23% of the time, Pallas kernels for 6%

profile of v1, /device:TPU:9, one launch (start us, length us, event | category | flops | bytes accessed | tf_op | source)
XLA Modules:
  0.0 986.8 jit_solution(17782677760116806087)
XLA Ops:
  24.1 32.4 %collective-permute-done.3 = bf16[272,408]{1,0:T(8,128)(2,1)} collective-permute-done((bf16[272,408]{1,0:T(8,128)(2,1)}, bf16[272,408]{1,0:T(8,128)(2,1)}, u32[]{:S(2)}, u32[]{:S(2)}) %collective-permute-start.3) | collective-permute-done | bytes 221984 | tf_op jit(solution)/shard_map/ppermute | solution.py:312
  69.5 8.9 collective-permute-done.8
  84.7 25.6 %collective-permute-done.13 = bf16[272,1224]{1,0:T(8,128)(2,1)} collective-permute-done((bf16[272,1224]{1,0:T(8,128)(2,1)}, bf16[272,1224]{1,0:T(8,128)(2,1)}, u32[]{:S(2)}, u32[]{:S(2)}) %collective-permute-start.13) | collective-permute-done | bytes 665888 | tf_op jit(solution)/shard_map/ppermute | solution.py:312
  143.2 11.9 %collective-permute-done.18 = bf16[1,608,1088]{1,2,0:T(8,128)(2,1)} collective-permute-done((bf16[1,608,1088]{1,2,0:T(8,128)(2,1)}, bf16[1,608,1088]{1,2,0:T(8,128)(2,1)}, u32[]{:S(2)}, u32[]{:S(2)}) %collective-permute-start.18) | collective-permute-done | bytes 1323040 | tf_op jit(solution)/shard_map/ppermute | solution.py:312
  163.6 12.0 %collective-permute-done.7 = bf16[2,208,1088]{2,1,0:T(8,128)(2,1)} collective-permute-done((bf16[2,208,1088]{2,1,0:T(8,128)(2,1)}, bf16[2,208,1088]{2,1,0:T(8,128)(2,1)}, u32[]{:S(2)}, u32[]{:S(2)}) %collective-permute-start.7) | collective-permute-done | bytes 905248 | tf_op jit(solution)/shard_map/ppermute | solution.py:312
  195.4 35.5 %collective-permute-done.19 = bf16[2,608,1088]{1,2,0:T(8,128)(2,1)} collective-permute-done((bf16[2,608,1088]{1,2,0:T(8,128)(2,1)}, bf16[2,608,1088]{1,2,0:T(8,128)(2,1)}, u32[]{:S(2)}, u32[]{:S(2)}) %collective-permute-start.19) | collective-permute-done | bytes 2646048 | tf_op jit(solution)/shard_map/ppermute | solution.py:312
  234.4 6.1 collective-permute-done.17
  243.6 8.2 pad_maximum_fusion.1
  260.3 5.9 pad_maximum_fusion.2
  289.6 5.4 collective-permute-start.23
  299.2 5.8 copy.199
  305.1 5.9 copy.200.refs_1_
  310.9 61.4 %attention_forward.1 = (bf16[2048,576]{1,0:T(8,128)(2,1)}, bf16[576,2048]{1,0:T(8,128)(2,1)}, f32[9,1,2048]{2,1,0:T(1,128)}) custom-call(s32[8]{0:T(128)} %and_select_fusion.first_ref, s32[2]{0:T(128)} %pad_add_fusion.2.part_ref, s32[1,2048]{1,0:T(1,128)} %bitcast.518, bf16[1024,1728]{1,0:T(8,128)(2,1)} %bitcast.478, bf16[1024,1728]{1,0:T(8,128)(2,1)} %copy.200.refs_1_), custom_call_target="tpu_custom_call" | custom-call | flops 12079595520 | bytes 11796480 | tf_op jit(solution)/shard_map/attention_forward/pallas_call | solution.py:213
  396.8 14.7 %select_bitcast_fusion.1 = (bf16[4,1,1224,1088]{2,3,1,0:T(8,128)(2,1)S(1)}, bf16[4,1,1224,1088]{2,3,1,0:T(8,128)(2,1)}) fusion(bf16[4,1224,1088]{1,2,0:T(8,128)(2,1)} %collective-permute-done.20, pred[]{:T(512)S(6)} %eq.67, bf16[4,608,1088]{1,2,0:T(8,128)(2,1)S(1)} %bitcast.443, bf16[4,616,1088]{1,2,0:T(8,128)(2,1)} %bitcast.445), kind=kLoop, calls=%fused_computation.15 | loop fusion | flops 31961088 | bytes 42614784 | tf_op jit(solution)/shard_map/stack | solution.py:399
  411.5 9.8 pad_maximum_fusion
  421.3 7.4 copy-done.3
  428.7 7.0 slice.186
  435.7 22.5 %fusion.129 = (bf16[8,136,1088]{1,2,0:T(8,128)(2,1)}, bf16[8,136,1088]{1,2,0:T(8,128)(2,1)}, bf16[8,136,1088]{1,2,0:T(8,128)(2,1)}, bf16[8,136,1088]{1,2,0:T(8,128)(2,1)}, bf16[8,136,1088]{1,2,0:T(8,128)(2,1)}) fusion(bf16[8,1224,1088]{1,2,0:T(8,128)(2,1)} %bitcast.433), kind=kLoop, calls=%fused_computation.339 | loop fusion | bytes 23674880 | tf_op jit(solution)/shard_map/slice | solution.py:421
  458.3 15.2 %copy.212 = bf16[8,544,1088]{2,1,0:T(8,128)(2,1)} copy(bf16[8,544,1088]{1,2,0:T(8,128)(2,1)} %slice.186) | data formatting | bytes 18939904 | tf_op jit(solution)/shard_map/slice | solution.py:414
  473.4 8.4 copy.213
  481.8 6.1 copy.216
  488.0 6.1 copy.219
  494.0 6.1 copy.218
  500.1 6.1 copy.217
  506.2 6.2 copy.211
  512.5 5.4 convert_add_fusion
  522.2 5.2 fusion.125
  527.4 5.6 fusion.124
  533.0 5.3 fusion.123
  538.3 5.2 fusion.126
  545.0 15.1 %fusion.136 = f32[1024,4352]{1,0:T(8,128)} fusion(bf16[1024,1088]{0,1:T(8,128)(2,1)S(1)} %multiply_convert_fusion.1, bf16[4352,1088]{1,0:T(8,128)(2,1)S(1)} %bitcast.460), kind=kOutput, calls=%fused_computation.346 | convolution fusion | flops 9697230848 | bytes 29523968 | tf_op jit(solution)/shard_map/dot_general | solution.py:21
  560.1 15.9 %multiply_convert_fusion = (bf16[1024,4352]{1,0:T(8,128)(2,1)}, f32[1024,4352]{1,0:T(8,128)}) fusion(f32[1024,4352]{1,0:T(8,128)} %fusion.136, bf16[1024,16]{0,1:T(8,128)(2,1)S(1)} %convolution_convert_fusion.13, bf16[16,4352]{1,0:T(8,128)(2,1)S(1)} %reshape.267), kind=kOutput, calls=%fused_computation.10 | convolution fusion | flops 187170816 | bytes 44736512 | tf_op jit(solution)/shard_map/dot_general | solution.py:25
  576.0 21.3 %concatenate.45 = f32[1024,4352]{1,0:T(8,128)} concatenate(f32[1024,1088]{1,0:T(8,128)} %fusion.126, f32[1024,1088]{1,0:T(8,128)} %fusion.125, f32[1024,1088]{1,0:T(8,128)} %fusion.124, f32[1024,1088]{1,0:T(8,128)} %fusion.123), dimensions={1} | concatenate | bytes 35651584 | tf_op jit(solution)/shard_map/concatenate | solution.py:510
  597.3 19.6 %fusion.6 = bf16[1024,4352]{1,0:T(8,128)(2,1)} fusion(f32[1024,4352]{1,0:T(8,128)} %get-tuple-element.126, f32[1024,4352]{1,0:T(8,128)} %concatenate.45, bf16[1024,16]{0,1:T(8,128)(2,1)S(1)} %copy-done.85, bf16[16,4352]{1,0:T(8,128)(2,1)S(1)} %copy-done.71), kind=kOutput, calls=%fused_computation.9 | convolution fusion | flops 236191744 | bytes 44736512 | tf_op jit(solution)/shard_map/dot_general | solution.py:25
  616.9 17.3 %fusion.137 = f32[1024,1088]{0,1:T(8,128)} fusion(bf16[1024,4352]{1,0:T(8,128)(2,1)} %fusion.6, bf16[4352,1088]{1,0:T(8,128)(2,1)} %bitcast.457), kind=kOutput, calls=%fused_computation.347 | convolution fusion | flops 9697230848 | bytes 22839296 | tf_op jit(solution)/shard_map/dot_general | solution.py:25
  634.3 6.1 convolution_convert_fusion.9
  701.9 72.3 %attention_backward.1 = bf16[2048,1728]{1,0:T(8,128)(2,1)} custom-call(s32[8]{0:T(128)} %and_select_fusion.first_ref, s32[2]{0:T(128)} %pad_add_fusion.2.part_ref, s32[1,2048]{1,0:T(1,128)} %bitcast.519, f32[9,1,2048]{2,1,0:T(1,128)} %get-tuple-element.14.lse_ref, bf16[576,2048]{1,0:T(8,128)(2,1)} %get-tuple-element.15.flipped_ref, ...), custom_call_target="tpu_custom_call" | custom-call | flops 30198988800 | bytes 18874368 | tf_op jit(solution)/shard_map/attention_backward/pallas_call | solution.py:243
  774.2 6.6 constant_dynamic-slice_fusion.6
  780.8 5.9 copy.230
  793.3 10.1 %fusion.26 = bf16[1024,1088]{0,1:T(8,128)(2,1)} fusion(f32[1024,1088]{0,1:T(8,128)} %copy-done.2, f32[1024,1088]{0,1:T(8,128)} %fusion.40, f32[1024,1088]{0,1:T(8,128)} %fusion.42, f32[1024,1088]{0,1:T(8,128)} %fusion.44, f32[1024,1088]{0,1:T(8,128)} %fusion.46, bf16[1024,16]{0,1:T(8,128)(2,1)S(1)} %convolution_convert_fusion.10, ...), kind=kOutput, calls=%fused_computation.64 | convolution fusion | flops 42336256 | bytes 24821764 | tf_op jit(solution)/shard_map/dot_general | solution.py:25
  803.4 5.3 reshape.274
  821.0 5.9 copy.253
  848.4 8.9 convolution_add_fusion.6
  865.1 5.3 reshape.277
  900.1 12.0 %collective-permute-done.21 = bf16[512,1088]{0,1:T(8,128)(2,1)S(1)} collective-permute-done((bf16[512,1088]{0,1:T(8,128)(2,1)S(1)}, bf16[512,1088]{0,1:T(8,128)(2,1)S(1)}, u32[]{:S(2)}, u32[]{:S(2)}) %collective-permute-start.21) | collective-permute-done | bytes 1114144 | tf_op jit(solution)/shard_map/ppermute | solution.py:312
  912.1 45.9 %collective-permute-done.22 = bf16[512,1088]{0,1:T(8,128)(2,1)S(1)} collective-permute-done((bf16[512,1088]{0,1:T(8,128)(2,1)S(1)}, bf16[512,1088]{0,1:T(8,128)(2,1)S(1)}, u32[]{:S(2)}, u32[]{:S(2)}) %collective-permute-start.22) | collective-permute-done | bytes 1114144 | tf_op jit(solution)/shard_map/ppermute | solution.py:312
  957.9 11.7 %collective-permute-done.27 = bf16[512,1088]{0,1:T(8,128)(2,1)S(1)} collective-permute-done((bf16[512,1088]{0,1:T(8,128)(2,1)S(1)}, bf16[512,1088]{0,1:T(8,128)(2,1)S(1)}, u32[]{:S(2)}, u32[]{:S(2)}) %collective-permute-start.27) | collective-permute-done | bytes 1114144 | tf_op jit(solution)/shard_map/ppermute | solution.py:312
  969.7 12.2 %collective-permute-done.28 = bf16[512,1088]{0,1:T(8,128)(2,1)S(1)} collective-permute-done((bf16[512,1088]{0,1:T(8,128)(2,1)S(1)}, bf16[512,1088]{0,1:T(8,128)(2,1)S(1)}, u32[]{:S(2)}, u32[]{:S(2)}) %collective-permute-start.28) | collective-permute-done | bytes 1114144 | tf_op jit(solution)/shard_map/ppermute | solution.py:312
  (517 shorter events, 318.0 us)
Async XLA Ops:
  0.7 56.8 %collective-permute-start.4 = (bf16[272,408]{1,0:T(8,128)(2,1)}, bf16[272,408]{1,0:T(8,128)(2,1)}, u32[]{:S(2)}, u32[]{:S(2)}) collective-permute-start(bf16[272,408]{1,0:T(8,128)(2,1)} %param.21), channel_id=1, source_target_pairs={{0,2},{1,3},{2,0},{3,1},{4,6},{5,7},{6,4},{7,5},{8,10},{9,11},{10,... | collective-permute-start | bytes 665864 | tf_op jit(solution)/shard_map/ppermute | solution.py:312
  3.0 53.5 %collective-permute-start.3 = (bf16[272,408]{1,0:T(8,128)(2,1)}, bf16[272,408]{1,0:T(8,128)(2,1)}, u32[]{:S(2)}, u32[]{:S(2)}) collective-permute-start(bf16[272,408]{1,0:T(8,128)(2,1)} %param.21), channel_id=1, source_target_pairs={{0,3},{1,0},{2,1},{3,2},{4,7},{5,4},{6,5},{7,6},{8,11},{9,8},{10,9... | collective-permute-start | bytes 665864 | tf_op jit(solution)/shard_map/ppermute | solution.py:312
  3.2 59.0 %collective-permute-start.5 = (bf16[272,408]{1,0:T(8,128)(2,1)}, bf16[272,408]{1,0:T(8,128)(2,1)}, u32[]{:S(2)}, u32[]{:S(2)}) collective-permute-start(bf16[272,408]{1,0:T(8,128)(2,1)} %param.21), channel_id=1, source_target_pairs={{0,1},{1,2},{2,3},{3,0},{4,5},{5,6},{6,7},{7,4},{8,9},{9,10},{10,1... | collective-permute-start | bytes 665864 | tf_op jit(solution)/shard_map/ppermute | solution.py:312
  6.0 12.7 %collective-permute-start.2 = (s32[2,2049]{1,0:T(2,128)S(1)}, s32[2,2049]{1,0:T(2,128)S(1)}, u32[]{:S(2)}, u32[]{:S(2)}) collective-permute-start(s32[2,2049]{1,0:T(2,128)S(1)} %pad_add_fusion), channel_id=1, source_target_pairs={{0,4},{1,5},{2,6},{3,7},{4,0},{5,1},{6,2},{7,3},{8,12},{9,13},{10,... | collective-permute-start | bytes 49184 | tf_op jit(solution)/shard_map/ppermute | solution.py:312
  17.1 97.0 %collective-permute-start.15 = (bf16[272,1224]{1,0:T(8,128)(2,1)}, bf16[272,1224]{1,0:T(8,128)(2,1)}, u32[]{:S(2)}, u32[]{:S(2)}) collective-permute-start(bf16[272,1224]{1,0:T(8,128)(2,1)} %concatenate.42), channel_id=1, source_target_pairs={{0,1},{1,2},{2,3},{3,0},{4,5},{5,6},{6,7},{7,4},{8,9},{9,10},{10,1... | collective-permute-start | bytes 1997576 | tf_op jit(solution)/shard_map/ppermute | solution.py:312
  18.7 93.7 %collective-permute-start.14 = (bf16[272,1224]{1,0:T(8,128)(2,1)}, bf16[272,1224]{1,0:T(8,128)(2,1)}, u32[]{:S(2)}, u32[]{:S(2)}) collective-permute-start(bf16[272,1224]{1,0:T(8,128)(2,1)} %concatenate.42), channel_id=1, source_target_pairs={{0,2},{1,3},{2,0},{3,1},{4,6},{5,7},{6,4},{7,5},{8,10},{9,11},{10,... | collective-permute-start | bytes 1997576 | tf_op jit(solution)/shard_map/ppermute | solution.py:312
  56.5 53.8 %collective-permute-start.13 = (bf16[272,1224]{1,0:T(8,128)(2,1)}, bf16[272,1224]{1,0:T(8,128)(2,1)}, u32[]{:S(2)}, u32[]{:S(2)}) collective-permute-start(bf16[272,1224]{1,0:T(8,128)(2,1)} %concatenate.42), channel_id=1, source_target_pairs={{0,3},{1,0},{2,1},{3,2},{4,7},{5,4},{6,5},{7,6},{8,11},{9,8},{10,9... | collective-permute-start | bytes 1997576 | tf_op jit(solution)/shard_map/ppermute | solution.py:312
  57.5 72.7 %collective-permute-start.1 = (bf16[512,1088]{0,1:T(8,128)(2,1)}, bf16[512,1088]{0,1:T(8,128)(2,1)}, u32[]{:S(2)}, u32[]{:S(2)}) collective-permute-start(bf16[512,1088]{0,1:T(8,128)(2,1)} %get-tuple-element.65), channel_id=1, source_target_pairs={{0,1},{1,0},{2,5},{3,4},{4,3},{5,2},{6,7},{7,6},{8,9},{9,8},{10,13... | collective-permute-start | bytes 3342344 | tf_op jit(solution)/shard_map/ppermute | solution.py:312
  66.8 11.6 %collective-permute-start.8 = (bf16[1,200,1088]{2,1,0:T(8,128)(2,1)S(1)}, bf16[1,200,1088]{2,1,0:T(8,128)(2,1)S(1)}, u32[]{:S(2)}, u32[]{:S(2)}) collective-permute-start(bf16[1,200,1088]{2,1,0:T(8,128)(2,1)S(1)} %copy.190), channel_id=1, source_target_pairs={{0,16},{1,17},{2,18},{3,19},{4,20},{5,21},{6,22},{7,23},{8,24},{9,... | collective-permute-start | bytes 1305608 | tf_op jit(solution)/shard_map/ppermute | solution.py:312
  78.4 56.7 %collective-permute-start = (bf16[512,1088]{0,1:T(8,128)(2,1)}, bf16[512,1088]{0,1:T(8,128)(2,1)}, u32[]{:S(2)}, u32[]{:S(2)}) collective-permute-start(bf16[512,1088]{0,1:T(8,128)(2,1)} %get-tuple-element.66), channel_id=1, source_target_pairs={{0,0},{1,1},{2,4},{3,5},{4,2},{5,3},{6,6},{7,7},{8,8},{9,9},{10,12... | collective-permute-start | bytes 3342344 | tf_op jit(solution)/shard_map/ppermute | solution.py:312
  110.3 14.0 %collective-permute-start.6 = (bf16[1,208,1088]{2,1,0:T(8,128)(2,1)S(1)}, bf16[1,208,1088]{2,1,0:T(8,128)(2,1)S(1)}, u32[]{:S(2)}, u32[]{:S(2)}) collective-permute-start(bf16[1,208,1088]{2,1,0:T(8,128)(2,1)S(1)} %copy-done.72), channel_id=1, source_target_pairs={{0,8},{1,9},{2,10},{3,11},{4,12},{5,13},{6,14},{7,15},{8,0},{9,1},... | collective-permute-start | bytes 1357832 | tf_op jit(solution)/shard_map/ppermute | solution.py:312
  112.4 29.0 %collective-permute-start.9 = (bf16[2,200,1088]{2,1,0:T(8,128)(2,1)}, bf16[2,200,1088]{2,1,0:T(8,128)(2,1)}, u32[]{:S(2)}, u32[]{:S(2)}) collective-permute-start(bf16[2,200,1088]{2,1,0:T(8,128)(2,1)} %copy.193), channel_id=1, source_target_pairs={{0,8},{1,9},{2,10},{3,11},{4,12},{5,13},{6,14},{7,15},{8,0},{9,1},... | collective-permute-start | bytes 2611208 | tf_op jit(solution)/shard_map/ppermute | solution.py:312
  123.3 53.8 %collective-permute-start.16 = (bf16[1,616,1088]{1,2,0:T(8,128)(2,1)}, bf16[1,616,1088]{1,2,0:T(8,128)(2,1)}, u32[]{:S(2)}, u32[]{:S(2)}) collective-permute-start(bf16[1,616,1088]{1,2,0:T(8,128)(2,1)} %slice_bitcast_fusion.1), channel_id=1, source_target_pairs={{0,8},{1,9},{2,10},{3,11},{4,12},{5,13},{6,14},{7,15},{8,0},{9,1},... | collective-permute-start | bytes 4021256 | tf_op jit(solution)/shard_map/ppermute | solution.py:312
  125.1 30.0 %collective-permute-start.18 = (bf16[1,608,1088]{1,2,0:T(8,128)(2,1)}, bf16[1,608,1088]{1,2,0:T(8,128)(2,1)}, u32[]{:S(2)}, u32[]{:S(2)}) collective-permute-start(bf16[1,608,1088]{1,2,0:T(8,128)(2,1)} %slice_bitcast_fusion), channel_id=1, source_target_pairs={{0,16},{1,17},{2,18},{3,19},{4,20},{5,21},{6,22},{7,23},{8,24},{9,... | collective-permute-start | bytes 3969032 | tf_op jit(solution)/shard_map/ppermute | solution.py:312
  130.2 45.4 %collective-permute-start.7 = (bf16[2,208,1088]{2,1,0:T(8,128)(2,1)}, bf16[2,208,1088]{2,1,0:T(8,128)(2,1)}, u32[]{:S(2)}, u32[]{:S(2)}) collective-permute-start(bf16[2,208,1088]{2,1,0:T(8,128)(2,1)} %copy.187), channel_id=1, source_target_pairs={{0,16},{1,17},{2,18},{3,19},{4,20},{5,21},{6,22},{7,23},{8,24},{9,... | collective-permute-start | bytes 2715656 | tf_op jit(solution)/shard_map/ppermute | solution.py:312
  160.0 70.9 %collective-permute-start.19 = (bf16[2,608,1088]{1,2,0:T(8,128)(2,1)}, bf16[2,608,1088]{1,2,0:T(8,128)(2,1)}, u32[]{:S(2)}, u32[]{:S(2)}) collective-permute-start(bf16[2,608,1088]{1,2,0:T(8,128)(2,1)} %maximum_bitcast_fusion.1), channel_id=1, source_target_pairs={{0,8},{1,9},{2,10},{3,11},{4,12},{5,13},{6,14},{7,15},{8,0},{9,1},... | collective-permute-start | bytes 7938056 | tf_op jit(solution)/shard_map/ppermute | solution.py:312
  181.6 58.9 %collective-permute-start.17 = (bf16[2,616,1088]{1,2,0:T(8,128)(2,1)}, bf16[2,616,1088]{1,2,0:T(8,128)(2,1)}, u32[]{:S(2)}, u32[]{:S(2)}) collective-permute-start(bf16[2,616,1088]{1,2,0:T(8,128)(2,1)} %maximum_bitcast_fusion), channel_id=1, source_target_pairs={{0,16},{1,17},{2,18},{3,19},{4,20},{5,21},{6,22},{7,23},{8,24},{9,... | collective-permute-start | bytes 8042504 | tf_op jit(solution)/shard_map/ppermute | solution.py:312
  191.8 64.2 %collective-permute-start.10 = (bf16[4,408,1088]{2,1,0:T(8,128)(2,1)}, bf16[4,408,1088]{2,1,0:T(8,128)(2,1)}, u32[]{:S(2)}, u32[]{:S(2)}) collective-permute-start(bf16[4,408,1088]{2,1,0:T(8,128)(2,1)} %pad_maximum_fusion.5), channel_id=1, source_target_pairs={{0,4},{1,5},{2,6},{3,7},{4,0},{5,1},{6,2},{7,3},{8,12},{9,13},{10,... | collective-permute-start | bytes 10653704 | tf_op jit(solution)/shard_map/ppermute | solution.py:312
  251.8 145.0 %collective-permute-start.20 = (bf16[4,1224,1088]{1,2,0:T(8,128)(2,1)}, bf16[4,1224,1088]{1,2,0:T(8,128)(2,1)}, u32[]{:S(2)}, u32[]{:S(2)}) collective-permute-start(bf16[4,1224,1088]{1,2,0:T(8,128)(2,1)} %pad_maximum_fusion.1), channel_id=1, source_target_pairs={{0,4},{1,5},{2,6},{3,7},{4,0},{5,1},{6,2},{7,3},{8,12},{9,13},{10,... | collective-permute-start | bytes 31961096 | tf_op jit(solution)/shard_map/ppermute | solution.py:312
  288.1 17.0 %collective-permute-start.11 = (bf16[1024,1728]{0,1:T(8,128)(2,1)}, bf16[1024,1728]{0,1:T(8,128)(2,1)}, u32[]{:S(2)}, u32[]{:S(2)}) collective-permute-start(bf16[1024,1728]{0,1:T(8,128)(2,1)} %get-tuple-element.35), channel_id=1, source_target_pairs={{0,4},{1,5},{2,6},{3,7},{4,0},{5,1},{6,2},{7,3},{8,12},{9,13},{10,... | collective-permute-start | bytes 10616840 | tf_op jit(solution)/shard_map/ppermute | solution.py:312
  289.6 98.0 %collective-permute-start.24 = (bf16[512,1088]{0,1:T(8,128)(2,1)}, bf16[512,1088]{0,1:T(8,128)(2,1)}, u32[]{:S(2)}, u32[]{:S(2)}) collective-permute-start(bf16[512,1088]{0,1:T(8,128)(2,1)} %get-tuple-element.57), channel_id=1, source_target_pairs={{0,1},{1,0},{2,5},{3,4},{4,3},{5,2},{6,7},{7,6},{8,9},{9,8},{10,13... | collective-permute-start | bytes 3342344 | tf_op jit(solution)/shard_map/ppermute | solution.py:312
  289.6 98.0 %collective-permute-start.23 = (bf16[512,1088]{0,1:T(8,128)(2,1)}, bf16[512,1088]{0,1:T(8,128)(2,1)}, u32[]{:S(2)}, u32[]{:S(2)}) collective-permute-start(bf16[512,1088]{0,1:T(8,128)(2,1)} %get-tuple-element.58), channel_id=1, source_target_pairs={{0,0},{1,1},{2,4},{3,5},{4,2},{5,3},{6,6},{7,7},{8,8},{9,9},{10,12... | collective-permute-start | bytes 3342344 | tf_op jit(solution)/shard_map/ppermute | solution.py:312
  375.8 16.9 %collective-permute-start.12 = (bf16[1024,576]{0,1:T(8,128)(2,1)}, bf16[1024,576]{0,1:T(8,128)(2,1)}, u32[]{:S(2)}, u32[]{:S(2)}) collective-permute-start(bf16[1024,576]{0,1:T(8,128)(2,1)} %bitcast.495), channel_id=1, source_target_pairs={{0,4},{1,5},{2,6},{3,7},{4,0},{5,1},{6,2},{7,3},{8,12},{9,13},{10,... | collective-permute-start | bytes 3538952 | tf_op jit(solution)/shard_map/ppermute | solution.py:312
  677.6 21.7 %collective-permute-start.41 = (bf16[16,3264]{1,0:T(8,128)(2,1)S(1)}, bf16[16,3264]{1,0:T(8,128)(2,1)S(1)}, u32[]{:S(2)}, u32[]{:S(2)}) collective-permute-start(bf16[16,3264]{1,0:T(8,128)(2,1)S(1)} %get-tuple-element.87), channel_id=1, source_target_pairs={{0,3},{1,0},{2,1},{3,2},{4,7},{5,4},{6,5},{7,6},{8,11},{9,8},{10,9... | collective-permute-start | bytes 313352 | tf_op jit(solution)/shard_map/ppermute | solution.py:312
  679.4 20.0 %collective-permute-start.40 = (bf16[16,3264]{1,0:T(8,128)(2,1)S(1)}, bf16[16,3264]{1,0:T(8,128)(2,1)S(1)}, u32[]{:S(2)}, u32[]{:S(2)}) collective-permute-start(bf16[16,3264]{1,0:T(8,128)(2,1)S(1)} %get-tuple-element.88), channel_id=1, source_target_pairs={{0,2},{1,3},{2,0},{3,1},{4,6},{5,7},{6,4},{7,5},{8,10},{9,11},{10,... | collective-permute-start | bytes 313352 | tf_op jit(solution)/shard_map/ppermute | solution.py:312
  681.6 17.9 %collective-permute-start.39 = (bf16[16,3264]{1,0:T(8,128)(2,1)S(1)}, bf16[16,3264]{1,0:T(8,128)(2,1)S(1)}, u32[]{:S(2)}, u32[]{:S(2)}) collective-permute-start(bf16[16,3264]{1,0:T(8,128)(2,1)S(1)} %get-tuple-element.89), channel_id=1, source_target_pairs={{0,1},{1,2},{2,3},{3,0},{4,5},{5,6},{6,7},{7,4},{8,9},{9,10},{10,1... | collective-permute-start | bytes 313352 | tf_op jit(solution)/shard_map/ppermute | solution.py:312
  686.2 13.3 %collective-permute-start.25 = (bf16[1024,576]{0,1:T(8,128)(2,1)S(1)}, bf16[1024,576]{0,1:T(8,128)(2,1)}, u32[]{:S(2)}, u32[]{:S(2)}) collective-permute-start(bf16[1024,576]{0,1:T(8,128)(2,1)S(1)} %get-tuple-element.47), channel_id=1, source_target_pairs={{0,4},{1,5},{2,6},{3,7},{4,0},{5,1},{6,2},{7,3},{8,12},{9,13},{10,... | collective-permute-start | bytes 3538952 | tf_op jit(solution)/shard_map/ppermute | solution.py:312
  786.8 40.1 %collective-permute-start.26 = (bf16[1024,1728]{0,1:T(8,128)(2,1)}, bf16[1024,1728]{0,1:T(8,128)(2,1)}, u32[]{:S(2)}, u32[]{:S(2)}) collective-permute-start(bf16[1024,1728]{0,1:T(8,128)(2,1)} %bitcast.480), channel_id=1, source_target_pairs={{0,4},{1,5},{2,6},{3,7},{4,0},{5,1},{6,2},{7,3},{8,12},{9,13},{10,... | collective-permute-start | bytes 10616840 | tf_op jit(solution)/shard_map/ppermute | solution.py:312
  790.5 19.7 %collective-permute-start.42 = (bf16[16,3264]{1,0:T(8,128)(2,1)S(1)}, bf16[16,3264]{1,0:T(8,128)(2,1)S(1)}, u32[]{:S(2)}, u32[]{:S(2)}) collective-permute-start(bf16[16,3264]{1,0:T(8,128)(2,1)S(1)} %get-tuple-element.79), channel_id=1, source_target_pairs={{0,4},{1,5},{2,6},{3,7},{4,0},{5,1},{6,2},{7,3},{8,12},{9,13},{10,... | collective-permute-start | bytes 313352 | tf_op jit(solution)/shard_map/ppermute | solution.py:312
  790.6 19.9 %collective-permute-start.48 = (bf16[16,3264]{1,0:T(8,128)(2,1)}, bf16[16,3264]{1,0:T(8,128)(2,1)S(1)}, u32[]{:S(2)}, u32[]{:S(2)}) collective-permute-start(bf16[16,3264]{1,0:T(8,128)(2,1)} %get-tuple-element.80), channel_id=1, source_target_pairs={{0,28},{1,29},{2,30},{3,31},{4,24},{5,25},{6,26},{7,27},{8,20},{9,... | collective-permute-start | bytes 313352 | tf_op jit(solution)/shard_map/ppermute | solution.py:312
  791.9 20.2 %collective-permute-start.47 = (bf16[16,3264]{1,0:T(8,128)(2,1)S(1)}, bf16[16,3264]{1,0:T(8,128)(2,1)S(1)}, u32[]{:S(2)}, u32[]{:S(2)}) collective-permute-start(bf16[16,3264]{1,0:T(8,128)(2,1)S(1)} %get-tuple-element.81), channel_id=1, source_target_pairs={{0,24},{1,25},{2,26},{3,27},{4,28},{5,29},{6,30},{7,31},{8,16},{9,... | collective-permute-start | bytes 313352 | tf_op jit(solution)/shard_map/ppermute | solution.py:312
  808.8 11.1 %collective-permute-start.46 = (bf16[16,3264]{1,0:T(8,128)(2,1)S(1)}, bf16[16,3264]{1,0:T(8,128)(2,1)S(1)}, u32[]{:S(2)}, u32[]{:S(2)}) collective-permute-start(bf16[16,3264]{1,0:T(8,128)(2,1)S(1)} %get-tuple-element.82), channel_id=1, source_target_pairs={{0,20},{1,21},{2,22},{3,23},{4,16},{5,17},{6,18},{7,19},{8,28},{9,... | collective-permute-start | bytes 313352 | tf_op jit(solution)/shard_map/ppermute | solution.py:312
  810.2 9.7 collective-permute-start.45
  810.5 9.4 collective-permute-start.44
  812.0 7.9 collective-permute-start.43
  844.7 25.8 %collective-permute-start.31 = (bf16[16,1088]{1,0:T(8,128)(2,1)S(1)}, bf16[16,1088]{1,0:T(8,128)(2,1)S(1)}, u32[]{:S(2)}, u32[]{:S(2)}) collective-permute-start(bf16[16,1088]{1,0:T(8,128)(2,1)S(1)} %bitcast.514), channel_id=1, source_target_pairs={{0,3},{1,0},{2,1},{3,2},{4,7},{5,4},{6,5},{7,6},{8,11},{9,8},{10,9... | collective-permute-start | bytes 104456 | tf_op jit(solution)/shard_map/ppermute | solution.py:312
  845.3 25.2 %collective-permute-start.30 = (bf16[16,1088]{1,0:T(8,128)(2,1)S(1)}, bf16[16,1088]{1,0:T(8,128)(2,1)S(1)}, u32[]{:S(2)}, u32[]{:S(2)}) collective-permute-start(bf16[16,1088]{1,0:T(8,128)(2,1)S(1)} %bitcast.513), channel_id=1, source_target_pairs={{0,2},{1,3},{2,0},{3,1},{4,6},{5,7},{6,4},{7,5},{8,10},{9,11},{10,... | collective-permute-start | bytes 104456 | tf_op jit(solution)/shard_map/ppermute | solution.py:312
  845.7 24.8 %collective-permute-start.29 = (bf16[16,1088]{1,0:T(8,128)(2,1)S(1)}, bf16[16,1088]{1,0:T(8,128)(2,1)S(1)}, u32[]{:S(2)}, u32[]{:S(2)}) collective-permute-start(bf16[16,1088]{1,0:T(8,128)(2,1)S(1)} %bitcast.512), channel_id=1, source_target_pairs={{0,1},{1,2},{2,3},{3,0},{4,5},{5,6},{6,7},{7,4},{8,9},{9,10},{10,1... | collective-permute-start | bytes 104456 | tf_op jit(solution)/shard_map/ppermute | solution.py:312
  870.9 10.9 %collective-permute-start.32 = (bf16[16,1088]{1,0:T(8,128)(2,1)S(1)}, bf16[16,1088]{1,0:T(8,128)(2,1)S(1)}, u32[]{:S(2)}, u32[]{:S(2)}) collective-permute-start(bf16[16,1088]{1,0:T(8,128)(2,1)S(1)} %get-tuple-element.96), channel_id=1, source_target_pairs={{0,4},{1,5},{2,6},{3,7},{4,0},{5,1},{6,2},{7,3},{8,12},{9,13},{10,... | collective-permute-start | bytes 104456 | tf_op jit(solution)/shard_map/ppermute | solution.py:312
  872.1 13.8 %collective-permute-start.38 = (bf16[16,1088]{1,0:T(8,128)(2,1)S(1)}, bf16[16,1088]{1,0:T(8,128)(2,1)S(1)}, u32[]{:S(2)}, u32[]{:S(2)}) collective-permute-start(bf16[16,1088]{1,0:T(8,128)(2,1)S(1)} %get-tuple-element.97), channel_id=1, source_target_pairs={{0,28},{1,29},{2,30},{3,31},{4,24},{5,25},{6,26},{7,27},{8,20},{9,... | collective-permute-start | bytes 104456 | tf_op jit(solution)/shard_map/ppermute | solution.py:312
  873.2 12.8 %collective-permute-start.37 = (bf16[16,1088]{1,0:T(8,128)(2,1)S(1)}, bf16[16,1088]{1,0:T(8,128)(2,1)S(1)}, u32[]{:S(2)}, u32[]{:S(2)}) collective-permute-start(bf16[16,1088]{1,0:T(8,128)(2,1)S(1)} %get-tuple-element.98), channel_id=1, source_target_pairs={{0,24},{1,25},{2,26},{3,27},{4,28},{5,29},{6,30},{7,31},{8,16},{9,... | collective-permute-start | bytes 104456 | tf_op jit(solution)/shard_map/ppermute | solution.py:312
  874.4 15.6 %collective-permute-start.36 = (bf16[16,1088]{1,0:T(8,128)(2,1)S(1)}, bf16[16,1088]{1,0:T(8,128)(2,1)S(1)}, u32[]{:S(2)}, u32[]{:S(2)}) collective-permute-start(bf16[16,1088]{1,0:T(8,128)(2,1)S(1)} %get-tuple-element.99), channel_id=1, source_target_pairs={{0,20},{1,21},{2,22},{3,23},{4,16},{5,17},{6,18},{7,19},{8,28},{9,... | collective-permute-start | bytes 104456 | tf_op jit(solution)/shard_map/ppermute | solution.py:312
  876.2 15.4 %collective-permute-start.35 = (bf16[16,1088]{1,0:T(8,128)(2,1)S(1)}, bf16[16,1088]{1,0:T(8,128)(2,1)S(1)}, u32[]{:S(2)}, u32[]{:S(2)}) collective-permute-start(bf16[16,1088]{1,0:T(8,128)(2,1)S(1)} %get-tuple-element.100), channel_id=1, source_target_pairs={{0,16},{1,17},{2,18},{3,19},{4,20},{5,21},{6,22},{7,23},{8,24},{9,... | collective-permute-start | bytes 104456 | tf_op jit(solution)/shard_map/ppermute | solution.py:312
  882.4 29.7 %collective-permute-start.21 = (bf16[512,1088]{0,1:T(8,128)(2,1)S(1)}, bf16[512,1088]{0,1:T(8,128)(2,1)S(1)}, u32[]{:S(2)}, u32[]{:S(2)}) collective-permute-start(bf16[512,1088]{0,1:T(8,128)(2,1)S(1)} %bitcast.501), channel_id=1, source_target_pairs={{0,0},{1,1},{2,4},{3,5},{4,2},{5,3},{6,6},{7,7},{8,8},{9,9},{10,12... | collective-permute-start | bytes 3342344 | tf_op jit(solution)/shard_map/ppermute | solution.py:312
  885.9 72.0 %collective-permute-start.22 = (bf16[512,1088]{0,1:T(8,128)(2,1)S(1)}, bf16[512,1088]{0,1:T(8,128)(2,1)S(1)}, u32[]{:S(2)}, u32[]{:S(2)}) collective-permute-start(bf16[512,1088]{0,1:T(8,128)(2,1)S(1)} %bitcast.500), channel_id=1, source_target_pairs={{0,1},{1,0},{2,5},{3,4},{4,3},{5,2},{6,7},{7,6},{8,9},{9,8},{10,13... | collective-permute-start | bytes 3342344 | tf_op jit(solution)/shard_map/ppermute | solution.py:312
  886.0 83.7 %collective-permute-start.27 = (bf16[512,1088]{0,1:T(8,128)(2,1)S(1)}, bf16[512,1088]{0,1:T(8,128)(2,1)S(1)}, u32[]{:S(2)}, u32[]{:S(2)}) collective-permute-start(bf16[512,1088]{0,1:T(8,128)(2,1)S(1)} %bitcast.503), channel_id=1, source_target_pairs={{0,0},{1,1},{2,4},{3,5},{4,2},{5,3},{6,6},{7,7},{8,8},{9,9},{10,12... | collective-permute-start | bytes 3342344 | tf_op jit(solution)/shard_map/ppermute | solution.py:312
  890.0 91.8 %collective-permute-start.28 = (bf16[512,1088]{0,1:T(8,128)(2,1)S(1)}, bf16[512,1088]{0,1:T(8,128)(2,1)S(1)}, u32[]{:S(2)}, u32[]{:S(2)}) collective-permute-start(bf16[512,1088]{0,1:T(8,128)(2,1)S(1)} %bitcast.502), channel_id=1, source_target_pairs={{0,1},{1,0},{2,5},{3,4},{4,3},{5,2},{6,7},{7,6},{8,9},{9,8},{10,13... | collective-permute-start | bytes 3342344 | tf_op jit(solution)/shard_map/ppermute | solution.py:312
  891.6 3.7 collective-permute-start.34
  (117 other events, 1284.8 us)
